TPU v7x, 32 devices: a whole 2x2x4 slice. The times are simulated.
32 devices in a mesh: row: 4 (over y, core), col: 8 (over z, x).
Axes of the slice: x: 2, y: 2, z: 4, core: 2. Of those that a mesh axis runs over, the one named last changes fastest.
Arguments:
- coeffs: float32 [2048, 2048], P('row', 'col'), may hold values from -8 to 8, as said below
- features: float32 [2048, 512], P('row'), may hold values from -0.6 to 0.6
- factors: float32 [2048, 256], P('row'), may hold values from -1.8 to 1.8
Outputs:
- grad_coeffs: float32 [2048, 2048], P('row', 'col')
- grad_features: float32 [2048, 512], P('row', 'col')
Inputs may be any that keep to these rules, and one draw needn't show every extreme that they name: `coeffs`: real coefficients.
All inputs are finite; a program needn't handle non-finite values.
Results may differ from a plain program's by a relative error of at most 0.0003.
Values sent between devices are 32-bit elements; how exact they have to be, the bound alone decides.
No kernel may reach another device: no remote copies, remote signals or barrier semaphores. Data moves between devices by JAX's collectives and lax.ppermute only.
A program may use at most 64 MiB of HBM per device.

v0:
```python
import functools
import jax
import jax.numpy as jnp
from jax import lax
from jax.experimental import pallas as pl
from jax.experimental.pallas import tpu as pltpu
from jax.sharding import PartitionSpec as P


AXES = ("row", "col")
F32, BF16 = jnp.float32, jnp.bfloat16


def split(value):
    high = value.astype(BF16)
    return high, (value - high.astype(F32)).astype(BF16)


def dot3(left, right, left_dim, right_dim):
    def one(a, b):
        return lax.dot_general(
            a, b, (((left_dim,), (right_dim,)), ((), ())), preferred_element_type=F32
        )

    return one(left[0], right[0]) + (one(left[0], right[1]) + one(left[1], right[0]))


def place(fold):
    col = lax.axis_index("col")
    return lax.axis_index("row"), lax.div(col, fold), lax.rem(col, fold)


def identity(first, shape):
    rows = lax.broadcasted_iota(jnp.int32, shape, 0)
    cols = lax.broadcasted_iota(jnp.int32, shape, 1)
    return jnp.where(rows - cols == first, 1.0, 0.0)


def rows_at(start, count):
    return pl.ds(pl.multiple_of(start, count), count)


def call(kernel, outs, args, scratch=(), flops=0, hbm=(), grant=2):
    moved = sum(4 * a.size for a in args) + sum(4 * o.size for o in outs)
    spaces = [pltpu.HBM if n in hbm else pltpu.VMEM for n in range(len(args))]
    return pl.pallas_call(
        kernel,
        out_shape=outs,
        in_specs=[pl.BlockSpec(memory_space=space) for space in spaces],
        out_specs=[pl.BlockSpec(memory_space=pltpu.VMEM) for _ in outs],
        scratch_shapes=list(scratch),
        compiler_params=pltpu.CompilerParams(vmem_limit_bytes=grant << 20),
        cost_estimate=pl.CostEstimate(flops=flops, bytes_accessed=moved, transcendentals=0),
    )(*args)


def shape(*dims, dtype=F32):
    return jax.ShapeDtypeStruct(dims, dtype)


def cut_kernel(cuts, fold, *refs):
    count = max(cut[0] for cut in cuts) + 1
    ins, outs, sems = refs[:count], refs[count:-1], refs[-1]
    r, q, b = place(fold)
    copies = []
    for n, (source, rows, block) in enumerate(cuts):
        copies.append(
            pltpu.make_async_copy(
                ins[source].at[rows_at(block(r, q, b) * rows, rows)], outs[n], sems.at[n]
            )
        )
    for copy in copies:
        copy.start()
    for copy in copies:
        copy.wait()


def cut_rows(arrays, cuts, fold):
    outs = [shape(rows, arrays[source].shape[1]) for source, rows, _ in cuts]
    return call(
        functools.partial(cut_kernel, cuts, fold),
        outs,
        arrays,
        scratch=[pltpu.SemaphoreType.DMA((len(cuts),))],
        hbm=range(len(arrays)),
    )


def residual_kernel(count, fold, *refs):
    parts, blocks, outs, total = refs[:count], refs[count : 2 * count], refs[2 * count : -1], refs[-1]
    r, q, b = place(fold)
    quarter, own_cols = parts[0].shape
    piece = quarter // fold
    for t in range(count):
        wanted = q ^ r ^ t
        left = parts[0][...]
        for s in range(1, count):
            left = jnp.where(wanted == s, parts[s][...], left)
        if t == 0:
            left = left - identity(b * own_cols - q * quarter, left.shape)
        product = dot3(split(left), split(blocks[t][...]), 1, 0)
        if t == 0:
            total[...] = product
        else:
            total[...] += product
    for d in range(fold):
        outs[d][...] = total[rows_at((b ^ d) * piece, piece)]


def assemble(chunks, high, low, fold, q, b):
    piece = chunks[0].shape[0]
    for n, chunk in enumerate(chunks):
        at = rows_at(((q ^ (n // fold)) * fold + (b ^ (n % fold))) * piece, piece)
        high[at], low[at] = split(chunk[...])


def add_kernel(left, right, out):
    out[...] = left[...] + right[...]


def pick_kernel(bit, fold, old_ref, got_ref, out):
    r, q, _ = place(fold)
    out[...] = jnp.where(((r ^ q) & (2 * bit - 1)) == bit, got_ref[...], old_ref[...])


def project_kernel(count, fold, *refs):
    chunks, coeffs = refs[: count * fold], refs[count * fold]
    give, keep, total, high, low = refs[count * fold + 1 :]
    r, q, b = place(fold)
    assemble(chunks, high, low, fold, q, b)
    own_rows, own_cols = coeffs.shape
    less_one = coeffs[...] - identity((q * fold + b) * own_cols - r * own_rows, coeffs.shape)
    total[...] = dot3((high[...], low[...]), split(less_one), 0, 0)
    half = give.shape[0]
    mine = r & 1
    give[...] = total[rows_at((1 - mine) * half, half)]
    keep[...] = total[rows_at(mine * half, half)]


def halve_kernel(bit, fold, flip, old_ref, got_ref, *refs):
    outs, total = refs[:-1], refs[-1]
    r, _, b = place(fold)
    total[...] = old_ref[...] + got_ref[...]
    pieces = len(outs) // 2
    rows = outs[0].shape[0]
    mine = lax.rem(lax.div(r, bit), 2)
    if flip:
        mine = 1 - mine
    for n, side in enumerate((1 - mine, mine)):
        for d in range(pieces):
            part = b ^ d if pieces > 1 else 0
            outs[n * pieces + d][...] = total[rows_at((side * pieces + part) * rows, rows)]


def join_kernel(fold, *refs):
    parts, out = refs[:-1], refs[-1]
    _, _, b = place(fold)
    cols = parts[0].shape[1]
    sums = [parts[2 * d][...] + parts[2 * d + 1][...] for d in range(fold)]
    for e in range(fold):
        value = sums[0]
        for d in range(1, fold):
            value = jnp.where((b ^ e) == d, sums[d], value)
        out[:, e * cols : (e + 1) * cols] = value


def coeff_kernel(count, fold, *refs):
    coeffs, factors, col_factors = refs[:3]
    blocks, mirrored = refs[3 : 3 + count], refs[3 + count : 3 + count + fold]
    chunks, (out, high, low) = refs[3 + count + fold : -3], refs[-3:]
    r, q, b = place(fold)
    assemble(chunks, high, low, fold, q, b)
    features = blocks[0][...]
    for t in range(1, count):
        features = jnp.where((r ^ q) == t, blocks[t][...], features)
    features = split(features)
    right = split(col_factors[...])
    rows = mirrored[0].shape[0]
    for e in range(fold):
        at = slice(e * rows, (e + 1) * rows)
        turned = mirrored[0][...]
        for d in range(1, fold):
            turned = jnp.where((b ^ e) == d, mirrored[d][...], turned)
        turned = turned.T
        own = coeffs[at]
        symmetric = 0.5 * (own * own + turned * turned)
        relation = symmetric - dot3(split(factors[at]), right, 1, 1)
        outer = dot3((high[at], low[at]), features, 1, 1)
        out[at] = outer + 2.0 * own * relation


def per_device(coeffs, features, factors):
    row_count = lax.axis_size("row")
    col_count = lax.axis_size("col")
    fold = col_count // row_count
    own_rows, own_cols = coeffs.shape
    width = features.shape[1]
    quarter = own_rows // row_count
    piece = quarter // fold
    bits = [1 << n for n in range(row_count.bit_length() - 1)]
    every, both = range(row_count), range(fold)

    def send(value, route):
        pairs = []
        for i in every:
            for j in every:
                for k in both:
                    to = route(i, j, k)
                    if to is not None:
                        start = i * col_count + j * fold + k
                        pairs.append((start, to[0] * col_count + to[1] * fold + to[2]))
        return lax.ppermute(value, AXES, pairs)

    b = lax.axis_index("col") % fold
    blocks = {0: lax.dynamic_slice_in_dim(features, b * own_cols, own_cols, 0)}
    for bit in reversed(bits):
        for t in list(blocks):
            blocks[t | bit] = send(blocks[t], lambda i, j, k: (i ^ bit, j, k))
    blocks = [blocks[t] for t in every]

    cuts = [(0, quarter, lambda r, q, b, s=s: q ^ s) for s in every]
    cuts += [(0, own_cols, lambda r, q, b, d=d: b ^ d) for d in both]
    cuts += [(1, own_cols, lambda r, q, b: b)]
    cut = cut_rows([coeffs, factors], cuts, fold)
    parts, turns, col_factors = cut[:row_count], cut[row_count:-1], cut[-1]
    parts = [send(parts[s], lambda i, j, k: (i, j ^ s, k)) if s else parts[s] for s in every]

    turns = [send(turns[d], lambda i, j, k: (i, j, k ^ d)) if d else turns[d] for d in both]

    mirrored = [send(turns[d], lambda i, j, k: (j, i, k)) for d in both]

    shares = call(
        functools.partial(residual_kernel, row_count, fold),
        [shape(piece, width)] * fold,
        [*parts, *blocks],
        scratch=[pltpu.VMEM((quarter, width), F32)],
        flops=6 * quarter * row_count * own_cols * width,
        grant=12,
    )
    share = shares[0]
    for d in range(1, fold):
        got = send(shares[d], lambda i, j, k: (i, j, k ^ d))
        share = call(add_kernel, [shape(piece, width)], [share, got])[0]

    for bit in reversed(bits):
        got = send(col_factors, lambda i, j, k: (i ^ bit, j, k))
        picked = functools.partial(pick_kernel, bit, fold)
        col_factors = call(picked, [shape(*got.shape)], [col_factors, got])[0]

    chunks = {0: share}
    for bit in reversed(bits):
        for s in list(chunks):
            chunks[s | bit] = send(chunks[s], lambda i, j, k: (i, j ^ bit, k))
    chunks = [chunks[s] for s in every]
    spread = []
    for s in every:
        for d in both:
            one = chunks[s]
            spread.append(send(one, lambda i, j, k: (i, j, k ^ d)) if d else one)

    halves = [pltpu.VMEM((own_rows, width), BF16)] * 2
    give, keep = call(
        functools.partial(project_kernel, row_count, fold),
        [shape(width // 2, own_cols)] * 2,
        [*spread, coeffs],
        scratch=[pltpu.VMEM((width, own_cols), F32), *halves],
        flops=6 * own_rows * own_cols * width,
        grant=12,
    )
    rows = width // 2
    for bit in bits[:-1]:
        got = send(give, lambda i, j, k: (i ^ bit, j, k))
        last = 2 * bit == bits[-1]
        count = fold if last else 1
        halved = call(
            functools.partial(halve_kernel, 2 * bit, fold, last),
            [shape(rows // (2 * count), own_cols)] * (2 * count),
            [keep, got],
            scratch=[pltpu.VMEM((rows, own_cols), F32)],
        )
        rows //= 2
        give, keep = halved[0], halved[1]
    gives, keeps = halved[:fold], halved[fold:]
    parts = []
    for d in both:
        far = bits[-1]
        parts += [
            send(keeps[d], lambda i, j, k: (i, j, k ^ d)) if d else keeps[d],
            send(gives[d], lambda i, j, k: (i ^ far, j, k ^ d)),
        ]
    joined = call(functools.partial(join_kernel, fold), [shape(rows // fold, own_rows)], parts)[0]

    def portion(i):
        out = 0
        for bit in bits:
            out = 2 * out + (i // bit) % 2
        return out ^ 1

    grad_features = send(joined, lambda i, j, k: (j, portion(i), k)).T

    grad_coeffs = call(
        functools.partial(coeff_kernel, row_count, fold),
        [shape(own_rows, own_cols)],
        [coeffs, factors, col_factors, *blocks, *mirrored, *spread],
        scratch=halves,
        flops=6 * own_rows * own_cols * (width + factors.shape[1]),
        grant=12,
    )[0]
    return (grad_coeffs, grad_features)


def solution(mesh):
    in_specs = (P("row", "col"), P("row", None), P("row", None))
    out_specs = (P("row", "col"), P("row", "col"))
    return jax.shard_map(
        per_device, mesh=mesh, in_specs=in_specs, out_specs=out_specs, check_vma=False
    )
```

profile of v0, /device:TPU:4, one launch (start us, length us, event | category | flops | bytes accessed | tf_op | source)
XLA Modules:
  0.0 94.3 jit_solution(4094060299006701799)
XLA Ops:
  0.7 1.2 %copy-done = f32[512,512]{1,0:T(8,128)S(1)} copy-done((f32[512,512]{1,0:T(8,128)S(1)}, f32[512,512]{1,0:T(8,128)}, u32[]{:S(2)}) %copy-start) | copy-done | bytes 1048600
  2.1 13.6 %collective-permute-done.3.refs_6_.refs_5_ = f32[256,512]{1,0:T(8,128)S(1)} collective-permute-done((f32[256,512]{1,0:T(8,128)S(1)}, f32[256,512]{1,0:T(8,128)S(1)}, u32[]{:S(2)}, u32[]{:S(2)}) %collective-permute-start.3) | collective-permute-done | bytes 524320 | tf_op jit(solution)/shard_map/ppermute | solution.py:212
  15.6 0.8 shard_map.50
  16.5 1.6 %collective-permute-start.8 = (f32[128,256]{1,0:T(8,128)S(1)}, f32[128,256]{1,0:T(8,128)S(1)}, u32[]{:S(2)}, u32[]{:S(2)}) collective-permute-start(f32[128,256]{1,0:T(8,128)S(1)} %get-tuple-element.21), channel_id=1, source_target_pairs={{0,2},{1,3},{2,0},{3,1},{4,6},{5,7},{6,4},{7,5},{8,10},{9,11},{10,... | collective-permute-start | bytes 393224 | tf_op jit(solution)/shard_map/ppermute | solution.py:212
  18.1 2.6 %collective-permute-start.9 = (f32[128,256]{1,0:T(8,128)S(1)}, f32[128,256]{1,0:T(8,128)S(1)}, u32[]{:S(2)}, u32[]{:S(2)}) collective-permute-start(f32[128,256]{1,0:T(8,128)S(1)} %get-tuple-element.22), channel_id=1, source_target_pairs={{0,4},{1,5},{2,6},{3,7},{4,0},{5,1},{6,2},{7,3},{8,12},{9,13},{10,... | collective-permute-start | bytes 393224 | tf_op jit(solution)/shard_map/ppermute | solution.py:212
  20.9 3.7 %collective-permute-done.8.refs_1_ = f32[128,256]{1,0:T(8,128)S(1)} collective-permute-done((f32[128,256]{1,0:T(8,128)S(1)}, f32[128,256]{1,0:T(8,128)S(1)}, u32[]{:S(2)}, u32[]{:S(2)}) %collective-permute-start.8) | collective-permute-done | bytes 131104 | tf_op jit(solution)/shard_map/ppermute | solution.py:212
  24.7 6.4 %collective-permute-done.9.refs_2_ = f32[128,256]{1,0:T(8,128)S(1)} collective-permute-done((f32[128,256]{1,0:T(8,128)S(1)}, f32[128,256]{1,0:T(8,128)S(1)}, u32[]{:S(2)}, u32[]{:S(2)}) %collective-permute-start.9) | collective-permute-done | bytes 131104 | tf_op jit(solution)/shard_map/ppermute | solution.py:212
  31.1 0.7 shard_map.53
  31.8 1.6 %collective-permute-start.11 = (f32[64,512]{1,0:T(8,128)S(1)}, f32[64,512]{1,0:T(8,128)S(1)}, u32[]{:S(2)}, u32[]{:S(2)}) collective-permute-start(f32[64,512]{1,0:T(8,128)S(1)} %get-tuple-element.25), channel_id=1, source_target_pairs={{0,1},{1,0},{2,3},{3,2},{4,5},{5,4},{6,7},{7,6},{8,9},{9,8},{10,11... | collective-permute-start | bytes 393224 | tf_op jit(solution)/shard_map/ppermute | solution.py:212
  33.4 3.5 %collective-permute-done.11.right = f32[64,512]{1,0:T(8,128)S(1)} collective-permute-done((f32[64,512]{1,0:T(8,128)S(1)}, f32[64,512]{1,0:T(8,128)S(1)}, u32[]{:S(2)}, u32[]{:S(2)}) %collective-permute-start.11) | collective-permute-done | bytes 131104 | tf_op jit(solution)/shard_map/ppermute | solution.py:212
  36.9 3.7 %collective-permute-start.15 = (f32[64,512]{1,0:T(8,128)S(1)}, f32[64,512]{1,0:T(8,128)S(1)}, u32[]{:S(2)}, u32[]{:S(2)}) collective-permute-start(f32[64,512]{1,0:T(8,128)S(1)} %shard_map.54.refs_9_.refs_0_), channel_id=1, source_target_pairs={{0,4},{1,5},{2,6},{3,7},{4,0},{5,1},{6,2},{7,3},{8,12},{9,13},{10,... | collective-permute-start | bytes 393224 | tf_op jit(solution)/shard_map/ppermute | solution.py:212
  40.5 4.8 %collective-permute-done.15.refs_13_.refs_4_ = f32[64,512]{1,0:T(8,128)S(1)} collective-permute-done((f32[64,512]{1,0:T(8,128)S(1)}, f32[64,512]{1,0:T(8,128)S(1)}, u32[]{:S(2)}, u32[]{:S(2)}) %collective-permute-start.15) | collective-permute-done | bytes 131104 | tf_op jit(solution)/shard_map/ppermute | solution.py:212
  45.5 1.5 %collective-permute-start.12 = (f32[64,512]{1,0:T(8,128)S(1)}, f32[64,512]{1,0:T(8,128)S(1)}, u32[]{:S(2)}, u32[]{:S(2)}) collective-permute-start(f32[64,512]{1,0:T(8,128)S(1)} %shard_map.54.refs_9_.refs_0_), channel_id=1, source_target_pairs={{0,1},{1,0},{2,3},{3,2},{4,5},{5,4},{6,7},{7,6},{8,9},{9,8},{10,11... | collective-permute-start | bytes 393224 | tf_op jit(solution)/shard_map/ppermute | solution.py:212
  47.0 0.5 collective-permute-start.16
  47.6 1.5 %collective-permute-start.14 = (f32[64,512]{1,0:T(8,128)S(1)}, f32[64,512]{1,0:T(8,128)S(1)}, u32[]{:S(2)}, u32[]{:S(2)}) collective-permute-start(f32[64,512]{1,0:T(8,128)S(1)} %collective-permute-done.13.refs_11_.refs_2_), channel_id=1, source_target_pairs={{0,1},{1,0},{2,3},{3,2},{4,5},{5,4},{6,7},{7,6},{8,9},{9,8},{10,11... | collective-permute-start | bytes 393224 | tf_op jit(solution)/shard_map/ppermute | solution.py:212
  49.1 1.2 %collective-permute-done.17.refs_15_.refs_6_ = f32[64,512]{1,0:T(8,128)S(1)} collective-permute-done((f32[64,512]{1,0:T(8,128)S(1)}, f32[64,512]{1,0:T(8,128)S(1)}, u32[]{:S(2)}, u32[]{:S(2)}) %collective-permute-start.17) | collective-permute-done | bytes 131104 | tf_op jit(solution)/shard_map/ppermute | solution.py:212
  50.3 1.5 %collective-permute-start.18 = (f32[64,512]{1,0:T(8,128)S(1)}, f32[64,512]{1,0:T(8,128)S(1)}, u32[]{:S(2)}, u32[]{:S(2)}) collective-permute-start(f32[64,512]{1,0:T(8,128)S(1)} %collective-permute-done.17.refs_15_.refs_6_), channel_id=1, source_target_pairs={{0,1},{1,0},{2,3},{3,2},{4,5},{5,4},{6,7},{7,6},{8,9},{9,8},{10,11... | collective-permute-start | bytes 393224 | tf_op jit(solution)/shard_map/ppermute | solution.py:212
  52.3 1.1 %collective-permute-start.6 = (f32[256,256]{1,0:T(8,128)S(1)}, f32[256,256]{1,0:T(8,128)S(1)}, u32[]{:S(2)}, u32[]{:S(2)}) collective-permute-start(f32[256,256]{1,0:T(8,128)S(1)} %get-tuple-element.19), channel_id=1, source_target_pairs={{0,1},{1,0},{2,3},{3,2},{4,5},{5,4},{6,7},{7,6},{8,9},{9,8},{10,11... | collective-permute-start | bytes 786440 | tf_op jit(solution)/shard_map/ppermute | solution.py:212
  53.4 1.3 %collective-permute-done.16.refs_14_.refs_5_ = f32[64,512]{1,0:T(8,128)S(1)} collective-permute-done((f32[64,512]{1,0:T(8,128)S(1)}, f32[64,512]{1,0:T(8,128)S(1)}, u32[]{:S(2)}, u32[]{:S(2)}) %collective-permute-start.16) | collective-permute-done | bytes 131104 | tf_op jit(solution)/shard_map/ppermute | solution.py:212
  54.7 2.8 %collective-permute-done.14.refs_12_.refs_3_ = f32[64,512]{1,0:T(8,128)S(1)} collective-permute-done((f32[64,512]{1,0:T(8,128)S(1)}, f32[64,512]{1,0:T(8,128)S(1)}, u32[]{:S(2)}, u32[]{:S(2)}) %collective-permute-start.14) | collective-permute-done | bytes 131104 | tf_op jit(solution)/shard_map/ppermute | solution.py:212
  57.5 1.8 %collective-permute-done.18.refs_16_.refs_7_ = f32[64,512]{1,0:T(8,128)S(1)} collective-permute-done((f32[64,512]{1,0:T(8,128)S(1)}, f32[64,512]{1,0:T(8,128)S(1)}, u32[]{:S(2)}, u32[]{:S(2)}) %collective-permute-start.18) | collective-permute-done | bytes 131104 | tf_op jit(solution)/shard_map/ppermute | solution.py:212
  59.4 0.9 shard_map.56
  60.4 0.5 collective-permute-start.1
  61.0 2.6 %collective-permute-start.5 = (f32[256,256]{1,0:T(8,128)S(1)}, f32[256,256]{1,0:T(8,128)S(1)}, u32[]{:S(2)}, u32[]{:S(2)}) collective-permute-start(f32[256,256]{1,0:T(8,128)S(1)} %get-tuple-element.18), channel_id=1, source_target_pairs={{0,0},{1,1},{2,8},{3,9},{4,16},{5,17},{6,24},{7,25},{8,2},{9,3},{1... | collective-permute-start | bytes 786440 | tf_op jit(solution)/shard_map/ppermute | solution.py:212
  63.6 5.0 %collective-permute-start.7 = (f32[256,256]{1,0:T(8,128)S(1)}, f32[256,256]{1,0:T(8,128)S(1)}, u32[]{:S(2)}, u32[]{:S(2)}) collective-permute-start(f32[256,256]{1,0:T(8,128)S(1)} %collective-permute-done.6), channel_id=1, source_target_pairs={{0,0},{1,1},{2,8},{3,9},{4,16},{5,17},{6,24},{7,25},{8,2},{9,3},{1... | collective-permute-start | bytes 786440 | tf_op jit(solution)/shard_map/ppermute | solution.py:212
  68.8 1.6 %collective-permute-start.21 = (f32[64,256]{1,0:T(8,128)S(1)}, f32[64,256]{1,0:T(8,128)S(1)}, u32[]{:S(2)}, u32[]{:S(2)}) collective-permute-start(f32[64,256]{1,0:T(8,128)S(1)} %get-tuple-element.30), channel_id=1, source_target_pairs={{0,1},{1,0},{2,3},{3,2},{4,5},{5,4},{6,7},{7,6},{8,9},{9,8},{10,11... | collective-permute-start | bytes 196616 | tf_op jit(solution)/shard_map/ppermute | solution.py:212
  70.3 4.5 %collective-permute-done.20.refs_1_ = f32[64,256]{1,0:T(8,128)S(1)} collective-permute-done((f32[64,256]{1,0:T(8,128)S(1)}, f32[64,256]{1,0:T(8,128)S(1)}, u32[]{:S(2)}, u32[]{:S(2)}) %collective-permute-start.20) | collective-permute-done | bytes 65568 | tf_op jit(solution)/shard_map/ppermute | solution.py:212
  75.1 5.4 %collective-permute-done.22.refs_3_ = f32[64,256]{1,0:T(8,128)S(1)} collective-permute-done((f32[64,256]{1,0:T(8,128)S(1)}, f32[64,256]{1,0:T(8,128)S(1)}, u32[]{:S(2)}, u32[]{:S(2)}) %collective-permute-start.22) | collective-permute-done | bytes 65568 | tf_op jit(solution)/shard_map/ppermute | solution.py:212
  80.7 5.7 %collective-permute-done.5.refs_7_ = f32[256,256]{1,0:T(8,128)S(1)} collective-permute-done((f32[256,256]{1,0:T(8,128)S(1)}, f32[256,256]{1,0:T(8,128)S(1)}, u32[]{:S(2)}, u32[]{:S(2)}) %collective-permute-start.5) | collective-permute-done | bytes 262176 | tf_op jit(solution)/shard_map/ppermute | solution.py:212
  86.5 5.3 %collective-permute-done.7.refs_8_ = f32[256,256]{1,0:T(8,128)S(1)} collective-permute-done((f32[256,256]{1,0:T(8,128)S(1)}, f32[256,256]{1,0:T(8,128)S(1)}, u32[]{:S(2)}, u32[]{:S(2)}) %collective-permute-start.7) | collective-permute-done | bytes 262176 | tf_op jit(solution)/shard_map/ppermute | solution.py:212
  91.8 1.9 %shard_map.55 = f32[512,256]{1,0:T(8,128)} custom-call(f32[512,256]{1,0:T(8,128)S(1)} %copy-done.1, f32[512,256]{1,0:T(8,128)S(1)} %copy-done.2, f32[256,256]{1,0:T(8,128)S(1)} %shard_map.52.refs_2_, f32[256,512]{1,0:T(8,128)S(1)} %constant_dynamic-slice_fusion.refs_4_.refs_3_, f32[256,512]{1,0:T(8,128)S(1)} %collective-permute-done.2.refs_5_.refs_4_, ...), custom_call_target="tpu_custom_call" | custom-call | flops 603979776 | bytes 5505024 | tf_op jit(solution)/shard_map/pallas_call | solution.py:46
  93.6 0.7 copy.6
  (33 shorter events, 1.9 us)
Async XLA Ops:
  0.6 1.2 %copy-start = (f32[512,512]{1,0:T(8,128)S(1)}, f32[512,512]{1,0:T(8,128)}, u32[]{:S(2)}) copy-start(f32[512,512]{1,0:T(8,128)} %param.4) | copy-start | bytes 3145732
  1.9 13.8 %copy-start.1 = (f32[512,256]{1,0:T(8,128)S(1)}, f32[512,256]{1,0:T(8,128)}, u32[]{:S(2)}) copy-start(f32[512,256]{1,0:T(8,128)} %refs_8_.1) | copy-start | bytes 1572868
  1.9 13.8 %copy-start.2 = (f32[512,256]{1,0:T(8,128)S(1)}, f32[512,256]{1,0:T(8,128)}, u32[]{:S(2)}) copy-start(f32[512,256]{1,0:T(8,128)} %refs_1_.3) | copy-start | bytes 1572868
  1.9 13.7 %collective-permute-start.3 = (f32[256,512]{1,0:T(8,128)S(1)}, f32[256,512]{1,0:T(8,128)S(1)}, u32[]{:S(2)}, u32[]{:S(2)}) collective-permute-start(f32[256,512]{1,0:T(8,128)S(1)} %constant_dynamic-slice_fusion.refs_4_.refs_3_), channel_id=1, source_target_pairs={{0,16},{1,17},{2,18},{3,19},{4,20},{5,21},{6,22},{7,23},{8,24},{9,... | collective-permute-start | bytes 1572872 | tf_op jit(solution)/shard_map/ppermute | solution.py:212
  2.0 29.1 %collective-permute-start.2 = (f32[256,512]{1,0:T(8,128)S(1)}, f32[256,512]{1,0:T(8,128)S(1)}, u32[]{:S(2)}, u32[]{:S(2)}) collective-permute-start(f32[256,512]{1,0:T(8,128)S(1)} %constant_dynamic-slice_fusion.refs_4_.refs_3_), channel_id=1, source_target_pairs={{0,8},{1,9},{2,10},{3,11},{4,12},{5,13},{6,14},{7,15},{8,0},{9,1},... | collective-permute-start | bytes 1572872 | tf_op jit(solution)/shard_map/ppermute | solution.py:212
  15.6 15.4 %collective-permute-start.4 = (f32[256,512]{1,0:T(8,128)S(1)}, f32[256,512]{1,0:T(8,128)S(1)}, u32[]{:S(2)}, u32[]{:S(2)}) collective-permute-start(f32[256,512]{1,0:T(8,128)S(1)} %collective-permute-done.3.refs_6_.refs_5_), channel_id=1, source_target_pairs={{0,8},{1,9},{2,10},{3,11},{4,12},{5,13},{6,14},{7,15},{8,0},{9,1},... | collective-permute-start | bytes 1572872 | tf_op jit(solution)/shard_map/ppermute | solution.py:212
  16.5 8.2 %collective-permute-start.8 = (f32[128,256]{1,0:T(8,128)S(1)}, f32[128,256]{1,0:T(8,128)S(1)}, u32[]{:S(2)}, u32[]{:S(2)}) collective-permute-start(f32[128,256]{1,0:T(8,128)S(1)} %get-tuple-element.21), channel_id=1, source_target_pairs={{0,2},{1,3},{2,0},{3,1},{4,6},{5,7},{6,4},{7,5},{8,10},{9,11},{10,... | collective-permute-start | bytes 393224 | tf_op jit(solution)/shard_map/ppermute | solution.py:212
  18.1 12.9 %collective-permute-start.9 = (f32[128,256]{1,0:T(8,128)S(1)}, f32[128,256]{1,0:T(8,128)S(1)}, u32[]{:S(2)}, u32[]{:S(2)}) collective-permute-start(f32[128,256]{1,0:T(8,128)S(1)} %get-tuple-element.22), channel_id=1, source_target_pairs={{0,4},{1,5},{2,6},{3,7},{4,0},{5,1},{6,2},{7,3},{8,12},{9,13},{10,... | collective-permute-start | bytes 393224 | tf_op jit(solution)/shard_map/ppermute | solution.py:212
  20.7 10.3 %collective-permute-start.10 = (f32[128,256]{1,0:T(8,128)S(1)}, f32[128,256]{1,0:T(8,128)S(1)}, u32[]{:S(2)}, u32[]{:S(2)}) collective-permute-start(f32[128,256]{1,0:T(8,128)S(1)} %get-tuple-element.23), channel_id=1, source_target_pairs={{0,6},{1,7},{2,4},{3,5},{4,2},{5,3},{6,0},{7,1},{8,14},{9,15},{10,... | collective-permute-start | bytes 393224 | tf_op jit(solution)/shard_map/ppermute | solution.py:212
  31.8 5.0 %collective-permute-start.11 = (f32[64,512]{1,0:T(8,128)S(1)}, f32[64,512]{1,0:T(8,128)S(1)}, u32[]{:S(2)}, u32[]{:S(2)}) collective-permute-start(f32[64,512]{1,0:T(8,128)S(1)} %get-tuple-element.25), channel_id=1, source_target_pairs={{0,1},{1,0},{2,3},{3,2},{4,5},{5,4},{6,7},{7,6},{8,9},{9,8},{10,11... | collective-permute-start | bytes 393224 | tf_op jit(solution)/shard_map/ppermute | solution.py:212
  36.9 8.5 %collective-permute-start.15 = (f32[64,512]{1,0:T(8,128)S(1)}, f32[64,512]{1,0:T(8,128)S(1)}, u32[]{:S(2)}, u32[]{:S(2)}) collective-permute-start(f32[64,512]{1,0:T(8,128)S(1)} %shard_map.54.refs_9_.refs_0_), channel_id=1, source_target_pairs={{0,4},{1,5},{2,6},{3,7},{4,0},{5,1},{6,2},{7,3},{8,12},{9,13},{10,... | collective-permute-start | bytes 393224 | tf_op jit(solution)/shard_map/ppermute | solution.py:212
  40.5 7.1 %collective-permute-start.13 = (f32[64,512]{1,0:T(8,128)S(1)}, f32[64,512]{1,0:T(8,128)S(1)}, u32[]{:S(2)}, u32[]{:S(2)}) collective-permute-start(f32[64,512]{1,0:T(8,128)S(1)} %shard_map.54.refs_9_.refs_0_), channel_id=1, source_target_pairs={{0,2},{1,3},{2,0},{3,1},{4,6},{5,7},{6,4},{7,5},{8,10},{9,11},{10,... | collective-permute-start | bytes 393224 | tf_op jit(solution)/shard_map/ppermute | solution.py:212
  45.3 5.0 %collective-permute-start.17 = (f32[64,512]{1,0:T(8,128)S(1)}, f32[64,512]{1,0:T(8,128)S(1)}, u32[]{:S(2)}, u32[]{:S(2)}) collective-permute-start(f32[64,512]{1,0:T(8,128)S(1)} %collective-permute-done.15.refs_13_.refs_4_), channel_id=1, source_target_pairs={{0,2},{1,3},{2,0},{3,1},{4,6},{5,7},{6,4},{7,5},{8,10},{9,11},{10,... | collective-permute-start | bytes 393224 | tf_op jit(solution)/shard_map/ppermute | solution.py:212
  45.5 6.8 %collective-permute-start.12 = (f32[64,512]{1,0:T(8,128)S(1)}, f32[64,512]{1,0:T(8,128)S(1)}, u32[]{:S(2)}, u32[]{:S(2)}) collective-permute-start(f32[64,512]{1,0:T(8,128)S(1)} %shard_map.54.refs_9_.refs_0_), channel_id=1, source_target_pairs={{0,1},{1,0},{2,3},{3,2},{4,5},{5,4},{6,7},{7,6},{8,9},{9,8},{10,11... | collective-permute-start | bytes 393224 | tf_op jit(solution)/shard_map/ppermute | solution.py:212
  47.0 7.7 %collective-permute-start.16 = (f32[64,512]{1,0:T(8,128)S(1)}, f32[64,512]{1,0:T(8,128)S(1)}, u32[]{:S(2)}, u32[]{:S(2)}) collective-permute-start(f32[64,512]{1,0:T(8,128)S(1)} %collective-permute-done.15.refs_13_.refs_4_), channel_id=1, source_target_pairs={{0,1},{1,0},{2,3},{3,2},{4,5},{5,4},{6,7},{7,6},{8,9},{9,8},{10,11... | collective-permute-start | bytes 393224 | tf_op jit(solution)/shard_map/ppermute | solution.py:212
  47.6 10.0 %collective-permute-start.14 = (f32[64,512]{1,0:T(8,128)S(1)}, f32[64,512]{1,0:T(8,128)S(1)}, u32[]{:S(2)}, u32[]{:S(2)}) collective-permute-start(f32[64,512]{1,0:T(8,128)S(1)} %collective-permute-done.13.refs_11_.refs_2_), channel_id=1, source_target_pairs={{0,1},{1,0},{2,3},{3,2},{4,5},{5,4},{6,7},{7,6},{8,9},{9,8},{10,11... | collective-permute-start | bytes 393224 | tf_op jit(solution)/shard_map/ppermute | solution.py:212
  50.3 9.1 %collective-permute-start.18 = (f32[64,512]{1,0:T(8,128)S(1)}, f32[64,512]{1,0:T(8,128)S(1)}, u32[]{:S(2)}, u32[]{:S(2)}) collective-permute-start(f32[64,512]{1,0:T(8,128)S(1)} %collective-permute-done.17.refs_15_.refs_6_), channel_id=1, source_target_pairs={{0,1},{1,0},{2,3},{3,2},{4,5},{5,4},{6,7},{7,6},{8,9},{9,8},{10,11... | collective-permute-start | bytes 393224 | tf_op jit(solution)/shard_map/ppermute | solution.py:212
  51.8 8.6 %collective-permute-start = (f32[256,256]{1,0:T(8,128)S(1)}, f32[256,256]{1,0:T(8,128)S(1)}, u32[]{:S(2)}, u32[]{:S(2)}) collective-permute-start(f32[256,256]{1,0:T(8,128)S(1)} %get-tuple-element.17.old_ref), channel_id=1, source_target_pairs={{0,16},{1,17},{2,18},{3,19},{4,20},{5,21},{6,22},{7,23},{8,24},{9,... | collective-permute-start | bytes 786440 | tf_op jit(solution)/shard_map/ppermute | solution.py:212
  52.3 11.3 %collective-permute-start.6 = (f32[256,256]{1,0:T(8,128)S(1)}, f32[256,256]{1,0:T(8,128)S(1)}, u32[]{:S(2)}, u32[]{:S(2)}) collective-permute-start(f32[256,256]{1,0:T(8,128)S(1)} %get-tuple-element.19), channel_id=1, source_target_pairs={{0,1},{1,0},{2,3},{3,2},{4,5},{5,4},{6,7},{7,6},{8,9},{9,8},{10,11... | collective-permute-start | bytes 786440 | tf_op jit(solution)/shard_map/ppermute | solution.py:212
  60.3 8.3 %collective-permute-start.19 = (f32[256,256]{1,0:T(8,128)S(1)}, f32[256,256]{1,0:T(8,128)S(1)}, u32[]{:S(2)}, u32[]{:S(2)}) collective-permute-start(f32[256,256]{1,0:T(8,128)S(1)} %get-tuple-element.27), channel_id=1, source_target_pairs={{0,8},{1,9},{2,10},{3,11},{4,12},{5,13},{6,14},{7,15},{8,0},{9,1},... | collective-permute-start | bytes 786440 | tf_op jit(solution)/shard_map/ppermute | solution.py:212
  60.4 20.3 %collective-permute-start.1 = (f32[256,256]{1,0:T(8,128)S(1)}, f32[256,256]{1,0:T(8,128)S(1)}, u32[]{:S(2)}, u32[]{:S(2)}) collective-permute-start(f32[256,256]{1,0:T(8,128)S(1)} %shard_map.51.old_ref), channel_id=1, source_target_pairs={{0,8},{1,9},{2,10},{3,11},{4,12},{5,13},{6,14},{7,15},{8,0},{9,1},... | collective-permute-start | bytes 786440 | tf_op jit(solution)/shard_map/ppermute | solution.py:212
  61.0 25.5 %collective-permute-start.5 = (f32[256,256]{1,0:T(8,128)S(1)}, f32[256,256]{1,0:T(8,128)S(1)}, u32[]{:S(2)}, u32[]{:S(2)}) collective-permute-start(f32[256,256]{1,0:T(8,128)S(1)} %get-tuple-element.18), channel_id=1, source_target_pairs={{0,0},{1,1},{2,8},{3,9},{4,16},{5,17},{6,24},{7,25},{8,2},{9,3},{1... | collective-permute-start | bytes 786440 | tf_op jit(solution)/shard_map/ppermute | solution.py:212
  63.6 28.2 %collective-permute-start.7 = (f32[256,256]{1,0:T(8,128)S(1)}, f32[256,256]{1,0:T(8,128)S(1)}, u32[]{:S(2)}, u32[]{:S(2)}) collective-permute-start(f32[256,256]{1,0:T(8,128)S(1)} %collective-permute-done.6), channel_id=1, source_target_pairs={{0,0},{1,1},{2,8},{3,9},{4,16},{5,17},{6,24},{7,25},{8,2},{9,3},{1... | collective-permute-start | bytes 786440 | tf_op jit(solution)/shard_map/ppermute | solution.py:212
  68.7 6.1 %collective-permute-start.20 = (f32[64,256]{1,0:T(8,128)S(1)}, f32[64,256]{1,0:T(8,128)S(1)}, u32[]{:S(2)}, u32[]{:S(2)}) collective-permute-start(f32[64,256]{1,0:T(8,128)S(1)} %get-tuple-element.29), channel_id=1, source_target_pairs={{0,16},{1,17},{2,18},{3,19},{4,20},{5,21},{6,22},{7,23},{8,24},{9,... | collective-permute-start | bytes 196616 | tf_op jit(solution)/shard_map/ppermute | solution.py:212
  68.8 6.4 %collective-permute-start.21 = (f32[64,256]{1,0:T(8,128)S(1)}, f32[64,256]{1,0:T(8,128)S(1)}, u32[]{:S(2)}, u32[]{:S(2)}) collective-permute-start(f32[64,256]{1,0:T(8,128)S(1)} %get-tuple-element.30), channel_id=1, source_target_pairs={{0,1},{1,0},{2,3},{3,2},{4,5},{5,4},{6,7},{7,6},{8,9},{9,8},{10,11... | collective-permute-start | bytes 196616 | tf_op jit(solution)/shard_map/ppermute | solution.py:212
  74.8 5.8 %collective-permute-start.22 = (f32[64,256]{1,0:T(8,128)S(1)}, f32[64,256]{1,0:T(8,128)S(1)}, u32[]{:S(2)}, u32[]{:S(2)}) collective-permute-start(f32[64,256]{1,0:T(8,128)S(1)} %get-tuple-element.31), channel_id=1, source_target_pairs={{0,17},{1,16},{2,19},{3,18},{4,21},{5,20},{6,23},{7,22},{8,25},{9,... | collective-permute-start | bytes 196616 | tf_op jit(solution)/shard_map/ppermute | solution.py:212
  80.6 13.1 %collective-permute-start.23 = (f32[64,512]{1,0:T(8,128)S(1)}, f32[64,512]{1,0:T(8,128)S(1)}, u32[]{:S(2)}, u32[]{:S(2)}) collective-permute-start(f32[64,512]{1,0:T(8,128)S(1)} %shard_map.58), channel_id=1, source_target_pairs={{0,2},{1,3},{2,10},{3,11},{4,18},{5,19},{6,26},{7,27},{8,6},{9,7},... | collective-permute-start | bytes 393224 | tf_op jit(solution)/shard_map/ppermute | solution.py:212
where the time goes:
time: 94.5 us; the launch traced here: 94.3 us
  waiting for transfers between devices  60.2 us (64%)
  starting transfers between devices  27 us (29%)
  Pallas kernels  4.47 us (5%)
  local copies, waits for them, and re-layouts  1.91 us (2%)
    ppermute x24, waiting for transfers between devices, send(): return lax.ppermute(value, AXES, pairs)  60.2 us
    ppermute x24, starting transfers between devices, send(): return lax.ppermute(value, AXES, pairs)  27 us
    pallas_call x9, Pallas kernels, call(): pl.pallas_call(kernel, out_shape=outs, in_specs=[pl.BlockSpec(memory_spac...  4.47 us
  transfers between devices with their start and end apart: 24, of which 13 were waited for; matrix products, arithmetic and copies ran while one was open for 0% of the time, Pallas kernels for 4%

commit v1 on v0

--- a/solution.py
+++ b/solution.py
@@ -166,8 +166,8 @@
 
 def coeff_kernel(count, fold, *refs):
     coeffs, factors, col_factors = refs[:3]
-    blocks, mirrored = refs[3 : 3 + count], refs[3 + count : 3 + count + fold]
-    chunks, (out, high, low) = refs[3 + count + fold : -3], refs[-3:]
+    blocks, mirrored = refs[3 : 3 + count], refs[3 + count : 4 + count + fold]
+    chunks, (out, high, low) = refs[4 + count + fold : -3], refs[-3:]
     r, q, b = place(fold)
     assemble(chunks, high, low, fold, q, b)
     features = blocks[0][...]
@@ -178,9 +178,10 @@
     rows = mirrored[0].shape[0]
     for e in range(fold):
         at = slice(e * rows, (e + 1) * rows)
-        turned = mirrored[0][...]
+        crossed = ((r ^ q) & (count // 2)) != 0
+        turned = jnp.where(crossed, mirrored[1][...], mirrored[0][...])
         for d in range(1, fold):
-            turned = jnp.where((b ^ e) == d, mirrored[d][...], turned)
+            turned = jnp.where((b ^ e) == d, mirrored[d + 1][...], turned)
         turned = turned.T
         own = coeffs[at]
         symmetric = 0.5 * (own * own + turned * turned)
@@ -227,7 +228,13 @@
 
     turns = [send(turns[d], lambda i, j, k: (i, j, k ^ d)) if d else turns[d] for d in both]
 
-    mirrored = [send(turns[d], lambda i, j, k: (j, i, k)) for d in both]
+    far = row_count // 2
+    hopped = send(turns[0], lambda i, j, k: (i ^ far, j, k))
+    mirrored = [
+        send(turns[0], lambda i, j, k: (i, j, k) if (i ^ j) & far else (j, i, k)),
+        send(hopped, lambda i, j, k: None if (i ^ j) & far else (j, i ^ far, k)),
+        *(send(turns[d], lambda i, j, k: (j, i, k)) for d in both if d),
+    ]
 
     shares = call(
         functools.partial(residual_kernel, row_count, fold),

time: 94.5 us -> 95.2 us (level)
  the two profiles are of different devices: /device:TPU:4 before, /device:TPU:1 now
where the time goes in v1:
time: 95.2 us; the launch traced here: 95 us
  waiting for transfers between devices  44.1 us (46%)
  starting transfers between devices  43.7 us (46%)
  Pallas kernels  4.47 us (5%)
  local copies, waits for them, and re-layouts  1.91 us (2%)
    ppermute x26, waiting for transfers between devices, send(): return lax.ppermute(value, AXES, pairs)  44.1 us
    ppermute x26, starting transfers between devices, send(): return lax.ppermute(value, AXES, pairs)  43.7 us
    pallas_call x9, Pallas kernels, call(): pl.pallas_call(kernel, out_shape=outs, in_specs=[pl.BlockSpec(memory_spac...  4.47 us
  transfers between devices with their start and end apart: 26, of which 13 were waited for; matrix products, arithmetic and copies ran while one was open for 0% of the time, Pallas kernels for 3%

profile of v1, /device:TPU:1, one launch (start us, length us, event | category | flops | bytes accessed | tf_op | source)
XLA Modules:
  0.0 95.0 jit_solution(13906715776462392370)
XLA Ops:
  0.7 1.2 %copy-done = f32[512,512]{1,0:T(8,128)S(1)} copy-done((f32[512,512]{1,0:T(8,128)S(1)}, f32[512,512]{1,0:T(8,128)}, u32[]{:S(2)}) %copy-start) | copy-done | bytes 1048600
  1.9 2.1 %collective-permute-start.3 = (f32[256,512]{1,0:T(8,128)S(1)}, f32[256,512]{1,0:T(8,128)S(1)}, u32[]{:S(2)}, u32[]{:S(2)}) collective-permute-start(f32[256,512]{1,0:T(8,128)S(1)} %constant_dynamic-slice_fusion.refs_4_.refs_3_), channel_id=1, source_target_pairs={{0,16},{1,17},{2,18},{3,19},{4,20},{5,21},{6,22},{7,23},{8,24},{9,... | collective-permute-start | bytes 1572872 | tf_op jit(solution)/shard_map/ppermute | solution.py:213
  5.0 10.7 %collective-permute-done.3.refs_6_.refs_5_ = f32[256,512]{1,0:T(8,128)S(1)} collective-permute-done((f32[256,512]{1,0:T(8,128)S(1)}, f32[256,512]{1,0:T(8,128)S(1)}, u32[]{:S(2)}, u32[]{:S(2)}) %collective-permute-start.3) | collective-permute-done | bytes 524320 | tf_op jit(solution)/shard_map/ppermute | solution.py:213
  15.7 1.3 %collective-permute-start.4 = (f32[256,512]{1,0:T(8,128)S(1)}, f32[256,512]{1,0:T(8,128)S(1)}, u32[]{:S(2)}, u32[]{:S(2)}) collective-permute-start(f32[256,512]{1,0:T(8,128)S(1)} %collective-permute-done.3.refs_6_.refs_5_), channel_id=1, source_target_pairs={{0,8},{1,9},{2,10},{3,11},{4,12},{5,13},{6,14},{7,15},{8,0},{9,1},... | collective-permute-start | bytes 1572872 | tf_op jit(solution)/shard_map/ppermute | solution.py:213
  17.7 1.6 %collective-permute-start.10 = (f32[128,256]{1,0:T(8,128)S(1)}, f32[128,256]{1,0:T(8,128)S(1)}, u32[]{:S(2)}, u32[]{:S(2)}) collective-permute-start(f32[128,256]{1,0:T(8,128)S(1)} %get-tuple-element.21), channel_id=1, source_target_pairs={{0,2},{1,3},{2,0},{3,1},{4,6},{5,7},{6,4},{7,5},{8,10},{9,11},{10,... | collective-permute-start | bytes 393224 | tf_op jit(solution)/shard_map/ppermute | solution.py:213
  19.3 2.3 %collective-permute-start.11 = (f32[128,256]{1,0:T(8,128)S(1)}, f32[128,256]{1,0:T(8,128)S(1)}, u32[]{:S(2)}, u32[]{:S(2)}) collective-permute-start(f32[128,256]{1,0:T(8,128)S(1)} %get-tuple-element.22), channel_id=1, source_target_pairs={{0,4},{1,5},{2,6},{3,7},{4,0},{5,1},{6,2},{7,3},{8,12},{9,13},{10,... | collective-permute-start | bytes 393224 | tf_op jit(solution)/shard_map/ppermute | solution.py:213
  21.6 1.3 %collective-permute-done.10.refs_1_ = f32[128,256]{1,0:T(8,128)S(1)} collective-permute-done((f32[128,256]{1,0:T(8,128)S(1)}, f32[128,256]{1,0:T(8,128)S(1)}, u32[]{:S(2)}, u32[]{:S(2)}) %collective-permute-start.10) | collective-permute-done | bytes 131104 | tf_op jit(solution)/shard_map/ppermute | solution.py:213
  22.9 2.1 %collective-permute-done.11.refs_2_ = f32[128,256]{1,0:T(8,128)S(1)} collective-permute-done((f32[128,256]{1,0:T(8,128)S(1)}, f32[128,256]{1,0:T(8,128)S(1)}, u32[]{:S(2)}, u32[]{:S(2)}) %collective-permute-start.11) | collective-permute-done | bytes 131104 | tf_op jit(solution)/shard_map/ppermute | solution.py:213
  25.0 5.7 %collective-permute-done.12.refs_3_ = f32[128,256]{1,0:T(8,128)S(1)} collective-permute-done((f32[128,256]{1,0:T(8,128)S(1)}, f32[128,256]{1,0:T(8,128)S(1)}, u32[]{:S(2)}, u32[]{:S(2)}) %collective-permute-start.12) | collective-permute-done | bytes 131104 | tf_op jit(solution)/shard_map/ppermute | solution.py:213
  31.4 1.3 %collective-permute-start.13 = (f32[64,512]{1,0:T(8,128)S(1)}, f32[64,512]{1,0:T(8,128)S(1)}, u32[]{:S(2)}, u32[]{:S(2)}) collective-permute-start(f32[64,512]{1,0:T(8,128)S(1)} %get-tuple-element.25), channel_id=1, source_target_pairs={{0,1},{1,0},{2,3},{3,2},{4,5},{5,4},{6,7},{7,6},{8,9},{9,8},{10,11... | collective-permute-start | bytes 393224 | tf_op jit(solution)/shard_map/ppermute | solution.py:213
  32.7 2.6 %collective-permute-done.13.right = f32[64,512]{1,0:T(8,128)S(1)} collective-permute-done((f32[64,512]{1,0:T(8,128)S(1)}, f32[64,512]{1,0:T(8,128)S(1)}, u32[]{:S(2)}, u32[]{:S(2)}) %collective-permute-start.13) | collective-permute-done | bytes 131104 | tf_op jit(solution)/shard_map/ppermute | solution.py:213
  35.4 4.1 %collective-permute-start.17 = (f32[64,512]{1,0:T(8,128)S(1)}, f32[64,512]{1,0:T(8,128)S(1)}, u32[]{:S(2)}, u32[]{:S(2)}) collective-permute-start(f32[64,512]{1,0:T(8,128)S(1)} %shard_map.54.refs_10_.refs_0_), channel_id=1, source_target_pairs={{0,4},{1,5},{2,6},{3,7},{4,0},{5,1},{6,2},{7,3},{8,12},{9,13},{10,... | collective-permute-start | bytes 393224 | tf_op jit(solution)/shard_map/ppermute | solution.py:213
  39.4 4.3 %collective-permute-done.17.refs_14_.refs_4_ = f32[64,512]{1,0:T(8,128)S(1)} collective-permute-done((f32[64,512]{1,0:T(8,128)S(1)}, f32[64,512]{1,0:T(8,128)S(1)}, u32[]{:S(2)}, u32[]{:S(2)}) %collective-permute-start.17) | collective-permute-done | bytes 131104 | tf_op jit(solution)/shard_map/ppermute | solution.py:213
  43.7 1.2 %collective-permute-start.14 = (f32[64,512]{1,0:T(8,128)S(1)}, f32[64,512]{1,0:T(8,128)S(1)}, u32[]{:S(2)}, u32[]{:S(2)}) collective-permute-start(f32[64,512]{1,0:T(8,128)S(1)} %shard_map.54.refs_10_.refs_0_), channel_id=1, source_target_pairs={{0,1},{1,0},{2,3},{3,2},{4,5},{5,4},{6,7},{7,6},{8,9},{9,8},{10,11... | collective-permute-start | bytes 393224 | tf_op jit(solution)/shard_map/ppermute | solution.py:213
  45.2 1.2 %collective-permute-start.16 = (f32[64,512]{1,0:T(8,128)S(1)}, f32[64,512]{1,0:T(8,128)S(1)}, u32[]{:S(2)}, u32[]{:S(2)}) collective-permute-start(f32[64,512]{1,0:T(8,128)S(1)} %collective-permute-done.15.refs_12_.refs_2_), channel_id=1, source_target_pairs={{0,1},{1,0},{2,3},{3,2},{4,5},{5,4},{6,7},{7,6},{8,9},{9,8},{10,11... | collective-permute-start | bytes 393224 | tf_op jit(solution)/shard_map/ppermute | solution.py:213
  46.4 1.5 %collective-permute-done.19.refs_16_.refs_6_ = f32[64,512]{1,0:T(8,128)S(1)} collective-permute-done((f32[64,512]{1,0:T(8,128)S(1)}, f32[64,512]{1,0:T(8,128)S(1)}, u32[]{:S(2)}, u32[]{:S(2)}) %collective-permute-start.19) | collective-permute-done | bytes 131104 | tf_op jit(solution)/shard_map/ppermute | solution.py:213
  47.9 1.2 %collective-permute-start.20 = (f32[64,512]{1,0:T(8,128)S(1)}, f32[64,512]{1,0:T(8,128)S(1)}, u32[]{:S(2)}, u32[]{:S(2)}) collective-permute-start(f32[64,512]{1,0:T(8,128)S(1)} %collective-permute-done.19.refs_16_.refs_6_), channel_id=1, source_target_pairs={{0,1},{1,0},{2,3},{3,2},{4,5},{5,4},{6,7},{7,6},{8,9},{9,8},{10,11... | collective-permute-start | bytes 393224 | tf_op jit(solution)/shard_map/ppermute | solution.py:213
  49.2 1.9 %collective-permute-done.16.refs_13_.refs_3_ = f32[64,512]{1,0:T(8,128)S(1)} collective-permute-done((f32[64,512]{1,0:T(8,128)S(1)}, f32[64,512]{1,0:T(8,128)S(1)}, u32[]{:S(2)}, u32[]{:S(2)}) %collective-permute-start.16) | collective-permute-done | bytes 131104 | tf_op jit(solution)/shard_map/ppermute | solution.py:213
  51.0 2.8 %collective-permute-done.20.refs_17_.refs_7_ = f32[64,512]{1,0:T(8,128)S(1)} collective-permute-done((f32[64,512]{1,0:T(8,128)S(1)}, f32[64,512]{1,0:T(8,128)S(1)}, u32[]{:S(2)}, u32[]{:S(2)}) %collective-permute-start.20) | collective-permute-done | bytes 131104 | tf_op jit(solution)/shard_map/ppermute | solution.py:213
  54.7 4.3 %collective-permute-start.21 = (f32[256,256]{1,0:T(8,128)S(1)}, f32[256,256]{1,0:T(8,128)S(1)}, u32[]{:S(2)}, u32[]{:S(2)}) collective-permute-start(f32[256,256]{1,0:T(8,128)S(1)} %get-tuple-element.27), channel_id=1, source_target_pairs={{0,8},{1,9},{2,10},{3,11},{4,12},{5,13},{6,14},{7,15},{8,0},{9,1},... | collective-permute-start | bytes 786440 | tf_op jit(solution)/shard_map/ppermute | solution.py:213
  59.0 1.2 %collective-permute-start = (f32[256,256]{1,0:T(8,128)S(1)}, f32[256,256]{1,0:T(8,128)S(1)}, u32[]{:S(2)}, u32[]{:S(2)}) collective-permute-start(f32[256,256]{1,0:T(8,128)S(1)} %get-tuple-element.17.old_ref), channel_id=1, source_target_pairs={{0,16},{1,17},{2,18},{3,19},{4,20},{5,21},{6,22},{7,23},{8,24},{9,... | collective-permute-start | bytes 786440 | tf_op jit(solution)/shard_map/ppermute | solution.py:213
  60.3 1.2 %collective-permute-start.8 = (f32[256,256]{1,0:T(8,128)S(1)}, f32[256,256]{1,0:T(8,128)S(1)}, u32[]{:S(2)}, u32[]{:S(2)}) collective-permute-start(f32[256,256]{1,0:T(8,128)S(1)} %get-tuple-element.19), channel_id=1, source_target_pairs={{0,1},{1,0},{2,3},{3,2},{4,5},{5,4},{6,7},{7,6},{8,9},{9,8},{10,11... | collective-permute-start | bytes 786440 | tf_op jit(solution)/shard_map/ppermute | solution.py:213
  61.8 1.3 %collective-permute-start.22 = (f32[64,256]{1,0:T(8,128)S(1)}, f32[64,256]{1,0:T(8,128)S(1)}, u32[]{:S(2)}, u32[]{:S(2)}) collective-permute-start(f32[64,256]{1,0:T(8,128)S(1)} %get-tuple-element.29), channel_id=1, source_target_pairs={{0,16},{1,17},{2,18},{3,19},{4,20},{5,21},{6,22},{7,23},{8,24},{9,... | collective-permute-start | bytes 196616 | tf_op jit(solution)/shard_map/ppermute | solution.py:213
  63.1 4.4 %collective-permute-start.5 = (f32[256,256]{1,0:T(8,128)S(1)}, f32[256,256]{1,0:T(8,128)S(1)}, u32[]{:S(2)}, u32[]{:S(2)}) collective-permute-start(f32[256,256]{1,0:T(8,128)S(1)} %get-tuple-element.18), channel_id=1, source_target_pairs={{0,0},{1,1},{2,8},{3,9},{4,4},{5,5},{6,6},{7,7},{8,2},{9,3},{10,10... | collective-permute-start | bytes 786440 | tf_op jit(solution)/shard_map/ppermute | solution.py:213
  68.4 3.8 %collective-permute-start.9 = (f32[256,256]{1,0:T(8,128)S(1)}, f32[256,256]{1,0:T(8,128)S(1)}, u32[]{:S(2)}, u32[]{:S(2)}) collective-permute-start(f32[256,256]{1,0:T(8,128)S(1)} %collective-permute-done.8), channel_id=1, source_target_pairs={{0,0},{1,1},{2,8},{3,9},{4,16},{5,17},{6,24},{7,25},{8,2},{9,3},{1... | collective-permute-start | bytes 786440 | tf_op jit(solution)/shard_map/ppermute | solution.py:213
  72.4 4.9 %collective-permute-start.7 = (f32[256,256]{1,0:T(8,128)S(1)}, f32[256,256]{1,0:T(8,128)S(1)}, u32[]{:S(2)}, u32[]{:S(2)}) collective-permute-start(f32[256,256]{1,0:T(8,128)S(1)} %collective-permute-done.6), channel_id=1, source_target_pairs={{0,4},{1,5},{2,12},{3,13},{8,6},{9,7},{10,14},{11,15},{20,16},{21,... | collective-permute-start | bytes 786440 | tf_op jit(solution)/shard_map/ppermute | solution.py:213
  77.4 1.3 %collective-permute-start.23 = (f32[64,256]{1,0:T(8,128)S(1)}, f32[64,256]{1,0:T(8,128)S(1)}, u32[]{:S(2)}, u32[]{:S(2)}) collective-permute-start(f32[64,256]{1,0:T(8,128)S(1)} %get-tuple-element.30), channel_id=1, source_target_pairs={{0,1},{1,0},{2,3},{3,2},{4,5},{5,4},{6,7},{7,6},{8,9},{9,8},{10,11... | collective-permute-start | bytes 196616 | tf_op jit(solution)/shard_map/ppermute | solution.py:213
  78.6 2.3 %collective-permute-done.23.refs_2_ = f32[64,256]{1,0:T(8,128)S(1)} collective-permute-done((f32[64,256]{1,0:T(8,128)S(1)}, f32[64,256]{1,0:T(8,128)S(1)}, u32[]{:S(2)}, u32[]{:S(2)}) %collective-permute-start.23) | collective-permute-done | bytes 65568 | tf_op jit(solution)/shard_map/ppermute | solution.py:213
  80.9 4.0 %collective-permute-done.24.refs_3_ = f32[64,256]{1,0:T(8,128)S(1)} collective-permute-done((f32[64,256]{1,0:T(8,128)S(1)}, f32[64,256]{1,0:T(8,128)S(1)}, u32[]{:S(2)}, u32[]{:S(2)}) %collective-permute-start.24) | collective-permute-done | bytes 65568 | tf_op jit(solution)/shard_map/ppermute | solution.py:213
  85.0 2.6 %collective-permute-start.25 = (f32[64,512]{1,0:T(8,128)S(1)}, f32[64,512]{1,0:T(8,128)S(1)}, u32[]{:S(2)}, u32[]{:S(2)}) collective-permute-start(f32[64,512]{1,0:T(8,128)S(1)} %shard_map.58), channel_id=1, source_target_pairs={{0,2},{1,3},{2,10},{3,11},{4,18},{5,19},{6,26},{7,27},{8,6},{9,7},... | collective-permute-start | bytes 393224 | tf_op jit(solution)/shard_map/ppermute | solution.py:213
  87.7 1.9 %shard_map.55 = f32[512,256]{1,0:T(8,128)} custom-call(f32[512,256]{1,0:T(8,128)S(1)} %copy-done.1, f32[512,256]{1,0:T(8,128)S(1)} %copy-done.2, f32[256,256]{1,0:T(8,128)S(1)} %shard_map.52.refs_2_, f32[256,512]{1,0:T(8,128)S(1)} %constant_dynamic-slice_fusion.refs_4_.refs_3_, f32[256,512]{1,0:T(8,128)S(1)} %collective-permute-done.2.refs_5_.refs_4_, ...), custom_call_target="tpu_custom_call" | custom-call | flops 603979776 | bytes 5767168 | tf_op jit(solution)/shard_map/pallas_call | solution.py:46
  89.6 4.7 %collective-permute-done.25 = f32[64,512]{1,0:T(8,128)S(1)} collective-permute-done((f32[64,512]{1,0:T(8,128)S(1)}, f32[64,512]{1,0:T(8,128)S(1)}, u32[]{:S(2)}, u32[]{:S(2)}) %collective-permute-start.25) | collective-permute-done | bytes 131104 | tf_op jit(solution)/shard_map/ppermute | solution.py:213
  (37 shorter events, 5.7 us)
Async XLA Ops:
  0.6 1.2 %copy-start = (f32[512,512]{1,0:T(8,128)S(1)}, f32[512,512]{1,0:T(8,128)}, u32[]{:S(2)}) copy-start(f32[512,512]{1,0:T(8,128)} %param.4) | copy-start | bytes 3145732
  1.9 15.0 %copy-start.1 = (f32[512,256]{1,0:T(8,128)S(1)}, f32[512,256]{1,0:T(8,128)}, u32[]{:S(2)}) copy-start(f32[512,256]{1,0:T(8,128)} %refs_8_.1) | copy-start | bytes 1572868
  1.9 15.0 %copy-start.2 = (f32[512,256]{1,0:T(8,128)S(1)}, f32[512,256]{1,0:T(8,128)}, u32[]{:S(2)}) copy-start(f32[512,256]{1,0:T(8,128)} %refs_1_.3) | copy-start | bytes 1572868
  1.9 13.8 %collective-permute-start.3 = (f32[256,512]{1,0:T(8,128)S(1)}, f32[256,512]{1,0:T(8,128)S(1)}, u32[]{:S(2)}, u32[]{:S(2)}) collective-permute-start(f32[256,512]{1,0:T(8,128)S(1)} %constant_dynamic-slice_fusion.refs_4_.refs_3_), channel_id=1, source_target_pairs={{0,16},{1,17},{2,18},{3,19},{4,20},{5,21},{6,22},{7,23},{8,24},{9,... | collective-permute-start | bytes 1572872 | tf_op jit(solution)/shard_map/ppermute | solution.py:213
  4.0 26.7 %collective-permute-start.2 = (f32[256,512]{1,0:T(8,128)S(1)}, f32[256,512]{1,0:T(8,128)S(1)}, u32[]{:S(2)}, u32[]{:S(2)}) collective-permute-start(f32[256,512]{1,0:T(8,128)S(1)} %constant_dynamic-slice_fusion.refs_4_.refs_3_), channel_id=1, source_target_pairs={{0,8},{1,9},{2,10},{3,11},{4,12},{5,13},{6,14},{7,15},{8,0},{9,1},... | collective-permute-start | bytes 1572872 | tf_op jit(solution)/shard_map/ppermute | solution.py:213
  15.7 15.1 %collective-permute-start.4 = (f32[256,512]{1,0:T(8,128)S(1)}, f32[256,512]{1,0:T(8,128)S(1)}, u32[]{:S(2)}, u32[]{:S(2)}) collective-permute-start(f32[256,512]{1,0:T(8,128)S(1)} %collective-permute-done.3.refs_6_.refs_5_), channel_id=1, source_target_pairs={{0,8},{1,9},{2,10},{3,11},{4,12},{5,13},{6,14},{7,15},{8,0},{9,1},... | collective-permute-start | bytes 1572872 | tf_op jit(solution)/shard_map/ppermute | solution.py:213
  17.7 5.2 %collective-permute-start.10 = (f32[128,256]{1,0:T(8,128)S(1)}, f32[128,256]{1,0:T(8,128)S(1)}, u32[]{:S(2)}, u32[]{:S(2)}) collective-permute-start(f32[128,256]{1,0:T(8,128)S(1)} %get-tuple-element.21), channel_id=1, source_target_pairs={{0,2},{1,3},{2,0},{3,1},{4,6},{5,7},{6,4},{7,5},{8,10},{9,11},{10,... | collective-permute-start | bytes 393224 | tf_op jit(solution)/shard_map/ppermute | solution.py:213
  19.3 5.7 %collective-permute-start.11 = (f32[128,256]{1,0:T(8,128)S(1)}, f32[128,256]{1,0:T(8,128)S(1)}, u32[]{:S(2)}, u32[]{:S(2)}) collective-permute-start(f32[128,256]{1,0:T(8,128)S(1)} %get-tuple-element.22), channel_id=1, source_target_pairs={{0,4},{1,5},{2,6},{3,7},{4,0},{5,1},{6,2},{7,3},{8,12},{9,13},{10,... | collective-permute-start | bytes 393224 | tf_op jit(solution)/shard_map/ppermute | solution.py:213
  21.6 9.1 %collective-permute-start.12 = (f32[128,256]{1,0:T(8,128)S(1)}, f32[128,256]{1,0:T(8,128)S(1)}, u32[]{:S(2)}, u32[]{:S(2)}) collective-permute-start(f32[128,256]{1,0:T(8,128)S(1)} %get-tuple-element.23), channel_id=1, source_target_pairs={{0,6},{1,7},{2,4},{3,5},{4,2},{5,3},{6,0},{7,1},{8,14},{9,15},{10,... | collective-permute-start | bytes 393224 | tf_op jit(solution)/shard_map/ppermute | solution.py:213
  31.4 3.9 %collective-permute-start.13 = (f32[64,512]{1,0:T(8,128)S(1)}, f32[64,512]{1,0:T(8,128)S(1)}, u32[]{:S(2)}, u32[]{:S(2)}) collective-permute-start(f32[64,512]{1,0:T(8,128)S(1)} %get-tuple-element.25), channel_id=1, source_target_pairs={{0,1},{1,0},{2,3},{3,2},{4,5},{5,4},{6,7},{7,6},{8,9},{9,8},{10,11... | collective-permute-start | bytes 393224 | tf_op jit(solution)/shard_map/ppermute | solution.py:213
  35.4 8.4 %collective-permute-start.17 = (f32[64,512]{1,0:T(8,128)S(1)}, f32[64,512]{1,0:T(8,128)S(1)}, u32[]{:S(2)}, u32[]{:S(2)}) collective-permute-start(f32[64,512]{1,0:T(8,128)S(1)} %shard_map.54.refs_10_.refs_0_), channel_id=1, source_target_pairs={{0,4},{1,5},{2,6},{3,7},{4,0},{5,1},{6,2},{7,3},{8,12},{9,13},{10,... | collective-permute-start | bytes 393224 | tf_op jit(solution)/shard_map/ppermute | solution.py:213
  39.4 5.8 %collective-permute-start.15 = (f32[64,512]{1,0:T(8,128)S(1)}, f32[64,512]{1,0:T(8,128)S(1)}, u32[]{:S(2)}, u32[]{:S(2)}) collective-permute-start(f32[64,512]{1,0:T(8,128)S(1)} %shard_map.54.refs_10_.refs_0_), channel_id=1, source_target_pairs={{0,2},{1,3},{2,0},{3,1},{4,6},{5,7},{6,4},{7,5},{8,10},{9,11},{10,... | collective-permute-start | bytes 393224 | tf_op jit(solution)/shard_map/ppermute | solution.py:213
  43.7 4.2 %collective-permute-start.19 = (f32[64,512]{1,0:T(8,128)S(1)}, f32[64,512]{1,0:T(8,128)S(1)}, u32[]{:S(2)}, u32[]{:S(2)}) collective-permute-start(f32[64,512]{1,0:T(8,128)S(1)} %collective-permute-done.17.refs_14_.refs_4_), channel_id=1, source_target_pairs={{0,2},{1,3},{2,0},{3,1},{4,6},{5,7},{6,4},{7,5},{8,10},{9,11},{10,... | collective-permute-start | bytes 393224 | tf_op jit(solution)/shard_map/ppermute | solution.py:213
  43.7 5.4 %collective-permute-start.14 = (f32[64,512]{1,0:T(8,128)S(1)}, f32[64,512]{1,0:T(8,128)S(1)}, u32[]{:S(2)}, u32[]{:S(2)}) collective-permute-start(f32[64,512]{1,0:T(8,128)S(1)} %shard_map.54.refs_10_.refs_0_), channel_id=1, source_target_pairs={{0,1},{1,0},{2,3},{3,2},{4,5},{5,4},{6,7},{7,6},{8,9},{9,8},{10,11... | collective-permute-start | bytes 393224 | tf_op jit(solution)/shard_map/ppermute | solution.py:213
  44.9 4.2 %collective-permute-start.18 = (f32[64,512]{1,0:T(8,128)S(1)}, f32[64,512]{1,0:T(8,128)S(1)}, u32[]{:S(2)}, u32[]{:S(2)}) collective-permute-start(f32[64,512]{1,0:T(8,128)S(1)} %collective-permute-done.17.refs_14_.refs_4_), channel_id=1, source_target_pairs={{0,1},{1,0},{2,3},{3,2},{4,5},{5,4},{6,7},{7,6},{8,9},{9,8},{10,11... | collective-permute-start | bytes 393224 | tf_op jit(solution)/shard_map/ppermute | solution.py:213
  45.2 5.9 %collective-permute-start.16 = (f32[64,512]{1,0:T(8,128)S(1)}, f32[64,512]{1,0:T(8,128)S(1)}, u32[]{:S(2)}, u32[]{:S(2)}) collective-permute-start(f32[64,512]{1,0:T(8,128)S(1)} %collective-permute-done.15.refs_12_.refs_2_), channel_id=1, source_target_pairs={{0,1},{1,0},{2,3},{3,2},{4,5},{5,4},{6,7},{7,6},{8,9},{9,8},{10,11... | collective-permute-start | bytes 393224 | tf_op jit(solution)/shard_map/ppermute | solution.py:213
  47.9 5.9 %collective-permute-start.20 = (f32[64,512]{1,0:T(8,128)S(1)}, f32[64,512]{1,0:T(8,128)S(1)}, u32[]{:S(2)}, u32[]{:S(2)}) collective-permute-start(f32[64,512]{1,0:T(8,128)S(1)} %collective-permute-done.19.refs_16_.refs_6_), channel_id=1, source_target_pairs={{0,1},{1,0},{2,3},{3,2},{4,5},{5,4},{6,7},{7,6},{8,9},{9,8},{10,11... | collective-permute-start | bytes 393224 | tf_op jit(solution)/shard_map/ppermute | solution.py:213
  54.7 7.0 %collective-permute-start.21 = (f32[256,256]{1,0:T(8,128)S(1)}, f32[256,256]{1,0:T(8,128)S(1)}, u32[]{:S(2)}, u32[]{:S(2)}) collective-permute-start(f32[256,256]{1,0:T(8,128)S(1)} %get-tuple-element.27), channel_id=1, source_target_pairs={{0,8},{1,9},{2,10},{3,11},{4,12},{5,13},{6,14},{7,15},{8,0},{9,1},... | collective-permute-start | bytes 786440 | tf_op jit(solution)/shard_map/ppermute | solution.py:213
  59.0 8.5 %collective-permute-start = (f32[256,256]{1,0:T(8,128)S(1)}, f32[256,256]{1,0:T(8,128)S(1)}, u32[]{:S(2)}, u32[]{:S(2)}) collective-permute-start(f32[256,256]{1,0:T(8,128)S(1)} %get-tuple-element.17.old_ref), channel_id=1, source_target_pairs={{0,16},{1,17},{2,18},{3,19},{4,20},{5,21},{6,22},{7,23},{8,24},{9,... | collective-permute-start | bytes 786440 | tf_op jit(solution)/shard_map/ppermute | solution.py:213
  60.3 8.1 %collective-permute-start.8 = (f32[256,256]{1,0:T(8,128)S(1)}, f32[256,256]{1,0:T(8,128)S(1)}, u32[]{:S(2)}, u32[]{:S(2)}) collective-permute-start(f32[256,256]{1,0:T(8,128)S(1)} %get-tuple-element.19), channel_id=1, source_target_pairs={{0,1},{1,0},{2,3},{3,2},{4,5},{5,4},{6,7},{7,6},{8,9},{9,8},{10,11... | collective-permute-start | bytes 786440 | tf_op jit(solution)/shard_map/ppermute | solution.py:213
  61.5 10.9 %collective-permute-start.6 = (f32[256,256]{1,0:T(8,128)S(1)}, f32[256,256]{1,0:T(8,128)S(1)}, u32[]{:S(2)}, u32[]{:S(2)}) collective-permute-start(f32[256,256]{1,0:T(8,128)S(1)} %get-tuple-element.18), channel_id=1, source_target_pairs={{0,16},{1,17},{2,18},{3,19},{4,20},{5,21},{6,22},{7,23},{8,24},{9,... | collective-permute-start | bytes 786440 | tf_op jit(solution)/shard_map/ppermute | solution.py:213
  61.8 15.6 %collective-permute-start.22 = (f32[64,256]{1,0:T(8,128)S(1)}, f32[64,256]{1,0:T(8,128)S(1)}, u32[]{:S(2)}, u32[]{:S(2)}) collective-permute-start(f32[64,256]{1,0:T(8,128)S(1)} %get-tuple-element.29), channel_id=1, source_target_pairs={{0,16},{1,17},{2,18},{3,19},{4,20},{5,21},{6,22},{7,23},{8,24},{9,... | collective-permute-start | bytes 196616 | tf_op jit(solution)/shard_map/ppermute | solution.py:213
  63.1 24.6 %collective-permute-start.5 = (f32[256,256]{1,0:T(8,128)S(1)}, f32[256,256]{1,0:T(8,128)S(1)}, u32[]{:S(2)}, u32[]{:S(2)}) collective-permute-start(f32[256,256]{1,0:T(8,128)S(1)} %get-tuple-element.18), channel_id=1, source_target_pairs={{0,0},{1,1},{2,8},{3,9},{4,4},{5,5},{6,6},{7,7},{8,2},{9,3},{10,10... | collective-permute-start | bytes 786440 | tf_op jit(solution)/shard_map/ppermute | solution.py:213
  67.6 20.0 %collective-permute-start.1 = (f32[256,256]{1,0:T(8,128)S(1)}, f32[256,256]{1,0:T(8,128)S(1)}, u32[]{:S(2)}, u32[]{:S(2)}) collective-permute-start(f32[256,256]{1,0:T(8,128)S(1)} %shard_map.51.old_ref), channel_id=1, source_target_pairs={{0,8},{1,9},{2,10},{3,11},{4,12},{5,13},{6,14},{7,15},{8,0},{9,1},... | collective-permute-start | bytes 786440 | tf_op jit(solution)/shard_map/ppermute | solution.py:213
  68.4 19.3 %collective-permute-start.9 = (f32[256,256]{1,0:T(8,128)S(1)}, f32[256,256]{1,0:T(8,128)S(1)}, u32[]{:S(2)}, u32[]{:S(2)}) collective-permute-start(f32[256,256]{1,0:T(8,128)S(1)} %collective-permute-done.8), channel_id=1, source_target_pairs={{0,0},{1,1},{2,8},{3,9},{4,16},{5,17},{6,24},{7,25},{8,2},{9,3},{1... | collective-permute-start | bytes 786440 | tf_op jit(solution)/shard_map/ppermute | solution.py:213
  72.4 15.2 %collective-permute-start.7 = (f32[256,256]{1,0:T(8,128)S(1)}, f32[256,256]{1,0:T(8,128)S(1)}, u32[]{:S(2)}, u32[]{:S(2)}) collective-permute-start(f32[256,256]{1,0:T(8,128)S(1)} %collective-permute-done.6), channel_id=1, source_target_pairs={{0,4},{1,5},{2,12},{3,13},{8,6},{9,7},{10,14},{11,15},{20,16},{21,... | collective-permute-start | bytes 786440 | tf_op jit(solution)/shard_map/ppermute | solution.py:213
  77.4 3.6 %collective-permute-start.23 = (f32[64,256]{1,0:T(8,128)S(1)}, f32[64,256]{1,0:T(8,128)S(1)}, u32[]{:S(2)}, u32[]{:S(2)}) collective-permute-start(f32[64,256]{1,0:T(8,128)S(1)} %get-tuple-element.30), channel_id=1, source_target_pairs={{0,1},{1,0},{2,3},{3,2},{4,5},{5,4},{6,7},{7,6},{8,9},{9,8},{10,11... | collective-permute-start | bytes 196616 | tf_op jit(solution)/shard_map/ppermute | solution.py:213
  80.9 4.0 %collective-permute-start.24 = (f32[64,256]{1,0:T(8,128)S(1)}, f32[64,256]{1,0:T(8,128)S(1)}, u32[]{:S(2)}, u32[]{:S(2)}) collective-permute-start(f32[64,256]{1,0:T(8,128)S(1)} %get-tuple-element.31), channel_id=1, source_target_pairs={{0,17},{1,16},{2,19},{3,18},{4,21},{5,20},{6,23},{7,22},{8,25},{9,... | collective-permute-start | bytes 196616 | tf_op jit(solution)/shard_map/ppermute | solution.py:213
  85.0 9.4 %collective-permute-start.25 = (f32[64,512]{1,0:T(8,128)S(1)}, f32[64,512]{1,0:T(8,128)S(1)}, u32[]{:S(2)}, u32[]{:S(2)}) collective-permute-start(f32[64,512]{1,0:T(8,128)S(1)} %shard_map.58), channel_id=1, source_target_pairs={{0,2},{1,3},{2,10},{3,11},{4,18},{5,19},{6,26},{7,27},{8,6},{9,7},... | collective-permute-start | bytes 393224 | tf_op jit(solution)/shard_map/ppermute | solution.py:213

commit v2 on v1

--- a/solution.py
+++ b/solution.py
@@ -124,13 +124,25 @@
 
 
 def project_kernel(count, fold, *refs):
-    chunks, coeffs = refs[: count * fold], refs[count * fold]
-    give, keep, total, high, low = refs[count * fold + 1 :]
-    r, q, b = place(fold)
+    chunks, coeffs = refs[: count * fold - 1], refs[count * fold - 1]
+    total, high, low = refs[count * fold :]
+    r, q, b = place(fold)
+    high[...] = jnp.zeros_like(high)
+    low[...] = jnp.zeros_like(low)
     assemble(chunks, high, low, fold, q, b)
     own_rows, own_cols = coeffs.shape
     less_one = coeffs[...] - identity((q * fold + b) * own_cols - r * own_rows, coeffs.shape)
     total[...] = dot3((high[...], low[...]), split(less_one), 0, 0)
+
+
+def last_kernel(count, fold, chunk, coeffs, part, give, keep, total):
+    r, q, b = place(fold)
+    own_rows, own_cols = coeffs.shape
+    piece = chunk.shape[0]
+    start = ((q ^ (count - 1)) * fold + (b ^ (fold - 1))) * piece
+    rows = coeffs[rows_at(start, piece)]
+    less_one = rows - identity((q * fold + b) * own_cols - r * own_rows - start, rows.shape)
+    total[...] = part[...] + dot3(split(chunk[...]), split(less_one), 0, 0)
     half = give.shape[0]
     mine = r & 1
     give[...] = total[rows_at((1 - mine) * half, half)]
@@ -232,7 +244,7 @@
     hopped = send(turns[0], lambda i, j, k: (i ^ far, j, k))
     mirrored = [
         send(turns[0], lambda i, j, k: (i, j, k) if (i ^ j) & far else (j, i, k)),
-        send(hopped, lambda i, j, k: None if (i ^ j) & far else (j, i ^ far, k)),
+        send(hopped, lambda i, j, k: (i ^ far, j, k) if (i ^ j) & far else (j, i ^ far, k)),
         *(send(turns[d], lambda i, j, k: (j, i, k)) for d in both if d),
     ]
 
@@ -266,13 +278,21 @@
             spread.append(send(one, lambda i, j, k: (i, j, k ^ d)) if d else one)
 
     halves = [pltpu.VMEM((own_rows, width), BF16)] * 2
-    give, keep = call(
+    part = call(
         functools.partial(project_kernel, row_count, fold),
-        [shape(width // 2, own_cols)] * 2,
-        [*spread, coeffs],
-        scratch=[pltpu.VMEM((width, own_cols), F32), *halves],
+        [shape(width, own_cols)],
+        [*spread[:-1], coeffs],
+        scratch=halves,
         flops=6 * own_rows * own_cols * width,
         grant=12,
+    )[0]
+    give, keep = call(
+        functools.partial(last_kernel, row_count, fold),
+        [shape(width // 2, own_cols)] * 2,
+        [spread[-1], coeffs, part],
+        scratch=[pltpu.VMEM((width, own_cols), F32)],
+        flops=6 * piece * own_cols * width,
+        grant=6,
     )
     rows = width // 2
     for bit in bits[:-1]:

time: 95.2 us -> 93.5 us (0.982)
  starting transfers between devices: 43.7 us -> 42.2 us
    ppermute x26, starting transfers between devices: 43.7 us -> 42.2 us  [send(): return lax.ppermute(value, AXES, pairs)]
    pallas_call x9 -> x10, Pallas kernels: 4.47 us -> 4.92 us  [call(): pl.pallas_call(kernel, out_shape=outs, in_specs=[pl.BlockSpec(memory_spac...]
  transfers between devices with their start and end apart: 26 -> 26, of which waited for: 13 -> 13; matrix products, arithmetic and copies ran while one was open for 0% -> 0% of each run, Pallas kernels for 3% -> 4%
where the time goes in v2:
time: 93.5 us; the launch traced here: 93.3 us
  waiting for transfers between devices  43.5 us (47%)
  starting transfers between devices  42.2 us (45%)
  Pallas kernels  4.92 us (5%)
  local copies, waits for them, and re-layouts  1.91 us (2%)
    ppermute x26, waiting for transfers between devices, send(): return lax.ppermute(value, AXES, pairs)  43.5 us
    ppermute x26, starting transfers between devices, send(): return lax.ppermute(value, AXES, pairs)  42.2 us
    pallas_call x10, Pallas kernels, call(): pl.pallas_call(kernel, out_shape=outs, in_specs=[pl.BlockSpec(memory_spac...  4.92 us
    unnamed x7, local copies, waits for them, and re-layouts  1.87 us
  transfers between devices with their start and end apart: 26, of which 13 were waited for; matrix products, arithmetic and copies ran while one was open for 0% of the time, Pallas kernels for 4%

profile of v2, /device:TPU:1, one launch (start us, length us, event | category | flops | bytes accessed | tf_op | source)
XLA Modules:
  0.0 93.3 jit_solution(16616524713277006727)
XLA Ops:
  0.7 1.2 %copy-done = f32[512,512]{1,0:T(8,128)S(1)} copy-done((f32[512,512]{1,0:T(8,128)S(1)}, f32[512,512]{1,0:T(8,128)}, u32[]{:S(2)}) %copy-start) | copy-done | bytes 1048600
  1.9 2.1 %collective-permute-start.3 = (f32[256,512]{1,0:T(8,128)S(1)}, f32[256,512]{1,0:T(8,128)S(1)}, u32[]{:S(2)}, u32[]{:S(2)}) collective-permute-start(f32[256,512]{1,0:T(8,128)S(1)} %constant_dynamic-slice_fusion.refs_4_.refs_3_), channel_id=1, source_target_pairs={{0,16},{1,17},{2,18},{3,19},{4,20},{5,21},{6,22},{7,23},{8,24},{9,... | collective-permute-start | bytes 1572872 | tf_op jit(solution)/shard_map/ppermute | solution.py:225
  5.0 10.7 %collective-permute-done.3.refs_6_.refs_5_ = f32[256,512]{1,0:T(8,128)S(1)} collective-permute-done((f32[256,512]{1,0:T(8,128)S(1)}, f32[256,512]{1,0:T(8,128)S(1)}, u32[]{:S(2)}, u32[]{:S(2)}) %collective-permute-start.3) | collective-permute-done | bytes 524320 | tf_op jit(solution)/shard_map/ppermute | solution.py:225
  15.7 1.3 %collective-permute-start.4 = (f32[256,512]{1,0:T(8,128)S(1)}, f32[256,512]{1,0:T(8,128)S(1)}, u32[]{:S(2)}, u32[]{:S(2)}) collective-permute-start(f32[256,512]{1,0:T(8,128)S(1)} %collective-permute-done.3.refs_6_.refs_5_), channel_id=1, source_target_pairs={{0,8},{1,9},{2,10},{3,11},{4,12},{5,13},{6,14},{7,15},{8,0},{9,1},... | collective-permute-start | bytes 1572872 | tf_op jit(solution)/shard_map/ppermute | solution.py:225
  17.7 1.6 %collective-permute-start.10 = (f32[128,256]{1,0:T(8,128)S(1)}, f32[128,256]{1,0:T(8,128)S(1)}, u32[]{:S(2)}, u32[]{:S(2)}) collective-permute-start(f32[128,256]{1,0:T(8,128)S(1)} %get-tuple-element.21), channel_id=1, source_target_pairs={{0,2},{1,3},{2,0},{3,1},{4,6},{5,7},{6,4},{7,5},{8,10},{9,11},{10,... | collective-permute-start | bytes 393224 | tf_op jit(solution)/shard_map/ppermute | solution.py:225
  19.3 2.3 %collective-permute-start.11 = (f32[128,256]{1,0:T(8,128)S(1)}, f32[128,256]{1,0:T(8,128)S(1)}, u32[]{:S(2)}, u32[]{:S(2)}) collective-permute-start(f32[128,256]{1,0:T(8,128)S(1)} %get-tuple-element.22), channel_id=1, source_target_pairs={{0,4},{1,5},{2,6},{3,7},{4,0},{5,1},{6,2},{7,3},{8,12},{9,13},{10,... | collective-permute-start | bytes 393224 | tf_op jit(solution)/shard_map/ppermute | solution.py:225
  21.6 1.3 %collective-permute-done.10.refs_1_ = f32[128,256]{1,0:T(8,128)S(1)} collective-permute-done((f32[128,256]{1,0:T(8,128)S(1)}, f32[128,256]{1,0:T(8,128)S(1)}, u32[]{:S(2)}, u32[]{:S(2)}) %collective-permute-start.10) | collective-permute-done | bytes 131104 | tf_op jit(solution)/shard_map/ppermute | solution.py:225
  22.9 2.1 %collective-permute-done.11.refs_2_ = f32[128,256]{1,0:T(8,128)S(1)} collective-permute-done((f32[128,256]{1,0:T(8,128)S(1)}, f32[128,256]{1,0:T(8,128)S(1)}, u32[]{:S(2)}, u32[]{:S(2)}) %collective-permute-start.11) | collective-permute-done | bytes 131104 | tf_op jit(solution)/shard_map/ppermute | solution.py:225
  25.0 5.7 %collective-permute-done.12.refs_3_ = f32[128,256]{1,0:T(8,128)S(1)} collective-permute-done((f32[128,256]{1,0:T(8,128)S(1)}, f32[128,256]{1,0:T(8,128)S(1)}, u32[]{:S(2)}, u32[]{:S(2)}) %collective-permute-start.12) | collective-permute-done | bytes 131104 | tf_op jit(solution)/shard_map/ppermute | solution.py:225
  31.4 1.3 %collective-permute-start.13 = (f32[64,512]{1,0:T(8,128)S(1)}, f32[64,512]{1,0:T(8,128)S(1)}, u32[]{:S(2)}, u32[]{:S(2)}) collective-permute-start(f32[64,512]{1,0:T(8,128)S(1)} %get-tuple-element.25), channel_id=1, source_target_pairs={{0,1},{1,0},{2,3},{3,2},{4,5},{5,4},{6,7},{7,6},{8,9},{9,8},{10,11... | collective-permute-start | bytes 393224 | tf_op jit(solution)/shard_map/ppermute | solution.py:225
  32.7 2.6 %collective-permute-done.13.right = f32[64,512]{1,0:T(8,128)S(1)} collective-permute-done((f32[64,512]{1,0:T(8,128)S(1)}, f32[64,512]{1,0:T(8,128)S(1)}, u32[]{:S(2)}, u32[]{:S(2)}) %collective-permute-start.13) | collective-permute-done | bytes 131104 | tf_op jit(solution)/shard_map/ppermute | solution.py:225
  35.4 4.1 %collective-permute-start.17 = (f32[64,512]{1,0:T(8,128)S(1)}, f32[64,512]{1,0:T(8,128)S(1)}, u32[]{:S(2)}, u32[]{:S(2)}) collective-permute-start(f32[64,512]{1,0:T(8,128)S(1)} %shard_map.54.refs_10_.refs_0_), channel_id=1, source_target_pairs={{0,4},{1,5},{2,6},{3,7},{4,0},{5,1},{6,2},{7,3},{8,12},{9,13},{10,... | collective-permute-start | bytes 393224 | tf_op jit(solution)/shard_map/ppermute | solution.py:225
  39.4 4.3 %collective-permute-done.17.refs_14_.refs_4_ = f32[64,512]{1,0:T(8,128)S(1)} collective-permute-done((f32[64,512]{1,0:T(8,128)S(1)}, f32[64,512]{1,0:T(8,128)S(1)}, u32[]{:S(2)}, u32[]{:S(2)}) %collective-permute-start.17) | collective-permute-done | bytes 131104 | tf_op jit(solution)/shard_map/ppermute | solution.py:225
  43.7 1.2 %collective-permute-start.14 = (f32[64,512]{1,0:T(8,128)S(1)}, f32[64,512]{1,0:T(8,128)S(1)}, u32[]{:S(2)}, u32[]{:S(2)}) collective-permute-start(f32[64,512]{1,0:T(8,128)S(1)} %shard_map.54.refs_10_.refs_0_), channel_id=1, source_target_pairs={{0,1},{1,0},{2,3},{3,2},{4,5},{5,4},{6,7},{7,6},{8,9},{9,8},{10,11... | collective-permute-start | bytes 393224 | tf_op jit(solution)/shard_map/ppermute | solution.py:225
  45.2 1.2 %collective-permute-start.16 = (f32[64,512]{1,0:T(8,128)S(1)}, f32[64,512]{1,0:T(8,128)S(1)}, u32[]{:S(2)}, u32[]{:S(2)}) collective-permute-start(f32[64,512]{1,0:T(8,128)S(1)} %collective-permute-done.15.refs_12_.refs_2_), channel_id=1, source_target_pairs={{0,1},{1,0},{2,3},{3,2},{4,5},{5,4},{6,7},{7,6},{8,9},{9,8},{10,11... | collective-permute-start | bytes 393224 | tf_op jit(solution)/shard_map/ppermute | solution.py:225
  46.4 1.5 %collective-permute-done.19.refs_16_.refs_6_ = f32[64,512]{1,0:T(8,128)S(1)} collective-permute-done((f32[64,512]{1,0:T(8,128)S(1)}, f32[64,512]{1,0:T(8,128)S(1)}, u32[]{:S(2)}, u32[]{:S(2)}) %collective-permute-start.19) | collective-permute-done | bytes 131104 | tf_op jit(solution)/shard_map/ppermute | solution.py:225
  47.9 1.2 %collective-permute-start.20 = (f32[64,512]{1,0:T(8,128)S(1)}, f32[64,512]{1,0:T(8,128)S(1)}, u32[]{:S(2)}, u32[]{:S(2)}) collective-permute-start(f32[64,512]{1,0:T(8,128)S(1)} %collective-permute-done.19.refs_16_.refs_6_), channel_id=1, source_target_pairs={{0,1},{1,0},{2,3},{3,2},{4,5},{5,4},{6,7},{7,6},{8,9},{9,8},{10,11... | collective-permute-start | bytes 393224 | tf_op jit(solution)/shard_map/ppermute | solution.py:225
  49.2 1.9 %collective-permute-done.16.refs_13_.refs_3_ = f32[64,512]{1,0:T(8,128)S(1)} collective-permute-done((f32[64,512]{1,0:T(8,128)S(1)}, f32[64,512]{1,0:T(8,128)S(1)}, u32[]{:S(2)}, u32[]{:S(2)}) %collective-permute-start.16) | collective-permute-done | bytes 131104 | tf_op jit(solution)/shard_map/ppermute | solution.py:225
  51.9 1.9 %collective-permute-done.20.refs_17_.chunk = f32[64,512]{1,0:T(8,128)S(1)} collective-permute-done((f32[64,512]{1,0:T(8,128)S(1)}, f32[64,512]{1,0:T(8,128)S(1)}, u32[]{:S(2)}, u32[]{:S(2)}) %collective-permute-start.20) | collective-permute-done | bytes 131104 | tf_op jit(solution)/shard_map/ppermute | solution.py:225
  54.3 4.3 %collective-permute-start.21 = (f32[256,256]{1,0:T(8,128)S(1)}, f32[256,256]{1,0:T(8,128)S(1)}, u32[]{:S(2)}, u32[]{:S(2)}) collective-permute-start(f32[256,256]{1,0:T(8,128)S(1)} %get-tuple-element.27), channel_id=1, source_target_pairs={{0,8},{1,9},{2,10},{3,11},{4,12},{5,13},{6,14},{7,15},{8,0},{9,1},... | collective-permute-start | bytes 786440 | tf_op jit(solution)/shard_map/ppermute | solution.py:225
  58.6 1.3 %collective-permute-start = (f32[256,256]{1,0:T(8,128)S(1)}, f32[256,256]{1,0:T(8,128)S(1)}, u32[]{:S(2)}, u32[]{:S(2)}) collective-permute-start(f32[256,256]{1,0:T(8,128)S(1)} %get-tuple-element.17.old_ref), channel_id=1, source_target_pairs={{0,16},{1,17},{2,18},{3,19},{4,20},{5,21},{6,22},{7,23},{8,24},{9,... | collective-permute-start | bytes 786440 | tf_op jit(solution)/shard_map/ppermute | solution.py:225
  59.8 1.2 %collective-permute-start.8 = (f32[256,256]{1,0:T(8,128)S(1)}, f32[256,256]{1,0:T(8,128)S(1)}, u32[]{:S(2)}, u32[]{:S(2)}) collective-permute-start(f32[256,256]{1,0:T(8,128)S(1)} %get-tuple-element.19), channel_id=1, source_target_pairs={{0,1},{1,0},{2,3},{3,2},{4,5},{5,4},{6,7},{7,6},{8,9},{9,8},{10,11... | collective-permute-start | bytes 786440 | tf_op jit(solution)/shard_map/ppermute | solution.py:225
  61.3 1.3 %collective-permute-start.22 = (f32[64,256]{1,0:T(8,128)S(1)}, f32[64,256]{1,0:T(8,128)S(1)}, u32[]{:S(2)}, u32[]{:S(2)}) collective-permute-start(f32[64,256]{1,0:T(8,128)S(1)} %get-tuple-element.29), channel_id=1, source_target_pairs={{0,16},{1,17},{2,18},{3,19},{4,20},{5,21},{6,22},{7,23},{8,24},{9,... | collective-permute-start | bytes 196616 | tf_op jit(solution)/shard_map/ppermute | solution.py:225
  62.6 4.4 %collective-permute-start.5 = (f32[256,256]{1,0:T(8,128)S(1)}, f32[256,256]{1,0:T(8,128)S(1)}, u32[]{:S(2)}, u32[]{:S(2)}) collective-permute-start(f32[256,256]{1,0:T(8,128)S(1)} %get-tuple-element.18), channel_id=1, source_target_pairs={{0,0},{1,1},{2,8},{3,9},{4,4},{5,5},{6,6},{7,7},{8,2},{9,3},{10,10... | collective-permute-start | bytes 786440 | tf_op jit(solution)/shard_map/ppermute | solution.py:225
  68.0 3.8 %collective-permute-start.9 = (f32[256,256]{1,0:T(8,128)S(1)}, f32[256,256]{1,0:T(8,128)S(1)}, u32[]{:S(2)}, u32[]{:S(2)}) collective-permute-start(f32[256,256]{1,0:T(8,128)S(1)} %collective-permute-done.8), channel_id=1, source_target_pairs={{0,0},{1,1},{2,8},{3,9},{4,16},{5,17},{6,24},{7,25},{8,2},{9,3},{1... | collective-permute-start | bytes 786440 | tf_op jit(solution)/shard_map/ppermute | solution.py:225
  72.0 3.0 %collective-permute-start.7 = (f32[256,256]{1,0:T(8,128)S(1)}, f32[256,256]{1,0:T(8,128)S(1)}, u32[]{:S(2)}, u32[]{:S(2)}) collective-permute-start(f32[256,256]{1,0:T(8,128)S(1)} %collective-permute-done.6), channel_id=1, source_target_pairs={{0,4},{1,5},{2,12},{3,13},{4,20},{5,21},{6,22},{7,23},{8,6},{9,7},... | collective-permute-start | bytes 786440 | tf_op jit(solution)/shard_map/ppermute | solution.py:225
  75.0 1.2 %collective-permute-start.23 = (f32[64,256]{1,0:T(8,128)S(1)}, f32[64,256]{1,0:T(8,128)S(1)}, u32[]{:S(2)}, u32[]{:S(2)}) collective-permute-start(f32[64,256]{1,0:T(8,128)S(1)} %get-tuple-element.30), channel_id=1, source_target_pairs={{0,1},{1,0},{2,3},{3,2},{4,5},{5,4},{6,7},{7,6},{8,9},{9,8},{10,11... | collective-permute-start | bytes 196616 | tf_op jit(solution)/shard_map/ppermute | solution.py:225
  76.2 2.7 %collective-permute-done.23.refs_2_ = f32[64,256]{1,0:T(8,128)S(1)} collective-permute-done((f32[64,256]{1,0:T(8,128)S(1)}, f32[64,256]{1,0:T(8,128)S(1)}, u32[]{:S(2)}, u32[]{:S(2)}) %collective-permute-start.23) | collective-permute-done | bytes 65568 | tf_op jit(solution)/shard_map/ppermute | solution.py:225
  79.0 4.3 %collective-permute-done.24.refs_3_ = f32[64,256]{1,0:T(8,128)S(1)} collective-permute-done((f32[64,256]{1,0:T(8,128)S(1)}, f32[64,256]{1,0:T(8,128)S(1)}, u32[]{:S(2)}, u32[]{:S(2)}) %collective-permute-start.24) | collective-permute-done | bytes 65568 | tf_op jit(solution)/shard_map/ppermute | solution.py:225
  83.3 3.1 %collective-permute-start.25 = (f32[64,512]{1,0:T(8,128)S(1)}, f32[64,512]{1,0:T(8,128)S(1)}, u32[]{:S(2)}, u32[]{:S(2)}) collective-permute-start(f32[64,512]{1,0:T(8,128)S(1)} %shard_map.59), channel_id=1, source_target_pairs={{0,2},{1,3},{2,10},{3,11},{4,18},{5,19},{6,26},{7,27},{8,6},{9,7},... | collective-permute-start | bytes 393224 | tf_op jit(solution)/shard_map/ppermute | solution.py:225
  86.5 1.9 %shard_map.55 = f32[512,256]{1,0:T(8,128)} custom-call(f32[512,256]{1,0:T(8,128)S(1)} %copy-done.1, f32[512,256]{1,0:T(8,128)S(1)} %copy-done.2, f32[256,256]{1,0:T(8,128)S(1)} %shard_map.52.refs_2_, f32[256,512]{1,0:T(8,128)S(1)} %constant_dynamic-slice_fusion.refs_4_.refs_3_, f32[256,512]{1,0:T(8,128)S(1)} %collective-permute-done.2.refs_5_.refs_4_, ...), custom_call_target="tpu_custom_call" | custom-call | flops 603979776 | bytes 5767168 | tf_op jit(solution)/shard_map/pallas_call | solution.py:46
  88.4 4.3 %collective-permute-done.25 = f32[64,512]{1,0:T(8,128)S(1)} collective-permute-done((f32[64,512]{1,0:T(8,128)S(1)}, f32[64,512]{1,0:T(8,128)S(1)}, u32[]{:S(2)}, u32[]{:S(2)}) %collective-permute-start.25) | collective-permute-done | bytes 131104 | tf_op jit(solution)/shard_map/ppermute | solution.py:225
  (38 shorter events, 6.2 us)
Async XLA Ops:
  0.6 1.2 %copy-start = (f32[512,512]{1,0:T(8,128)S(1)}, f32[512,512]{1,0:T(8,128)}, u32[]{:S(2)}) copy-start(f32[512,512]{1,0:T(8,128)} %param.4) | copy-start | bytes 3145732
  1.9 15.0 %copy-start.1 = (f32[512,256]{1,0:T(8,128)S(1)}, f32[512,256]{1,0:T(8,128)}, u32[]{:S(2)}) copy-start(f32[512,256]{1,0:T(8,128)} %coeffs.1) | copy-start | bytes 1572868
  1.9 15.0 %copy-start.2 = (f32[512,256]{1,0:T(8,128)S(1)}, f32[512,256]{1,0:T(8,128)}, u32[]{:S(2)}) copy-start(f32[512,256]{1,0:T(8,128)} %refs_1_.3) | copy-start | bytes 1572868
  1.9 13.8 %collective-permute-start.3 = (f32[256,512]{1,0:T(8,128)S(1)}, f32[256,512]{1,0:T(8,128)S(1)}, u32[]{:S(2)}, u32[]{:S(2)}) collective-permute-start(f32[256,512]{1,0:T(8,128)S(1)} %constant_dynamic-slice_fusion.refs_4_.refs_3_), channel_id=1, source_target_pairs={{0,16},{1,17},{2,18},{3,19},{4,20},{5,21},{6,22},{7,23},{8,24},{9,... | collective-permute-start | bytes 1572872 | tf_op jit(solution)/shard_map/ppermute | solution.py:225
  4.0 26.7 %collective-permute-start.2 = (f32[256,512]{1,0:T(8,128)S(1)}, f32[256,512]{1,0:T(8,128)S(1)}, u32[]{:S(2)}, u32[]{:S(2)}) collective-permute-start(f32[256,512]{1,0:T(8,128)S(1)} %constant_dynamic-slice_fusion.refs_4_.refs_3_), channel_id=1, source_target_pairs={{0,8},{1,9},{2,10},{3,11},{4,12},{5,13},{6,14},{7,15},{8,0},{9,1},... | collective-permute-start | bytes 1572872 | tf_op jit(solution)/shard_map/ppermute | solution.py:225
  15.7 15.1 %collective-permute-start.4 = (f32[256,512]{1,0:T(8,128)S(1)}, f32[256,512]{1,0:T(8,128)S(1)}, u32[]{:S(2)}, u32[]{:S(2)}) collective-permute-start(f32[256,512]{1,0:T(8,128)S(1)} %collective-permute-done.3.refs_6_.refs_5_), channel_id=1, source_target_pairs={{0,8},{1,9},{2,10},{3,11},{4,12},{5,13},{6,14},{7,15},{8,0},{9,1},... | collective-permute-start | bytes 1572872 | tf_op jit(solution)/shard_map/ppermute | solution.py:225
  17.7 5.2 %collective-permute-start.10 = (f32[128,256]{1,0:T(8,128)S(1)}, f32[128,256]{1,0:T(8,128)S(1)}, u32[]{:S(2)}, u32[]{:S(2)}) collective-permute-start(f32[128,256]{1,0:T(8,128)S(1)} %get-tuple-element.21), channel_id=1, source_target_pairs={{0,2},{1,3},{2,0},{3,1},{4,6},{5,7},{6,4},{7,5},{8,10},{9,11},{10,... | collective-permute-start | bytes 393224 | tf_op jit(solution)/shard_map/ppermute | solution.py:225
  19.3 5.7 %collective-permute-start.11 = (f32[128,256]{1,0:T(8,128)S(1)}, f32[128,256]{1,0:T(8,128)S(1)}, u32[]{:S(2)}, u32[]{:S(2)}) collective-permute-start(f32[128,256]{1,0:T(8,128)S(1)} %get-tuple-element.22), channel_id=1, source_target_pairs={{0,4},{1,5},{2,6},{3,7},{4,0},{5,1},{6,2},{7,3},{8,12},{9,13},{10,... | collective-permute-start | bytes 393224 | tf_op jit(solution)/shard_map/ppermute | solution.py:225
  21.6 9.1 %collective-permute-start.12 = (f32[128,256]{1,0:T(8,128)S(1)}, f32[128,256]{1,0:T(8,128)S(1)}, u32[]{:S(2)}, u32[]{:S(2)}) collective-permute-start(f32[128,256]{1,0:T(8,128)S(1)} %get-tuple-element.23), channel_id=1, source_target_pairs={{0,6},{1,7},{2,4},{3,5},{4,2},{5,3},{6,0},{7,1},{8,14},{9,15},{10,... | collective-permute-start | bytes 393224 | tf_op jit(solution)/shard_map/ppermute | solution.py:225
  31.4 3.9 %collective-permute-start.13 = (f32[64,512]{1,0:T(8,128)S(1)}, f32[64,512]{1,0:T(8,128)S(1)}, u32[]{:S(2)}, u32[]{:S(2)}) collective-permute-start(f32[64,512]{1,0:T(8,128)S(1)} %get-tuple-element.25), channel_id=1, source_target_pairs={{0,1},{1,0},{2,3},{3,2},{4,5},{5,4},{6,7},{7,6},{8,9},{9,8},{10,11... | collective-permute-start | bytes 393224 | tf_op jit(solution)/shard_map/ppermute | solution.py:225
  35.4 8.4 %collective-permute-start.17 = (f32[64,512]{1,0:T(8,128)S(1)}, f32[64,512]{1,0:T(8,128)S(1)}, u32[]{:S(2)}, u32[]{:S(2)}) collective-permute-start(f32[64,512]{1,0:T(8,128)S(1)} %shard_map.54.refs_10_.refs_0_), channel_id=1, source_target_pairs={{0,4},{1,5},{2,6},{3,7},{4,0},{5,1},{6,2},{7,3},{8,12},{9,13},{10,... | collective-permute-start | bytes 393224 | tf_op jit(solution)/shard_map/ppermute | solution.py:225
  39.4 5.8 %collective-permute-start.15 = (f32[64,512]{1,0:T(8,128)S(1)}, f32[64,512]{1,0:T(8,128)S(1)}, u32[]{:S(2)}, u32[]{:S(2)}) collective-permute-start(f32[64,512]{1,0:T(8,128)S(1)} %shard_map.54.refs_10_.refs_0_), channel_id=1, source_target_pairs={{0,2},{1,3},{2,0},{3,1},{4,6},{5,7},{6,4},{7,5},{8,10},{9,11},{10,... | collective-permute-start | bytes 393224 | tf_op jit(solution)/shard_map/ppermute | solution.py:225
  43.7 4.2 %collective-permute-start.19 = (f32[64,512]{1,0:T(8,128)S(1)}, f32[64,512]{1,0:T(8,128)S(1)}, u32[]{:S(2)}, u32[]{:S(2)}) collective-permute-start(f32[64,512]{1,0:T(8,128)S(1)} %collective-permute-done.17.refs_14_.refs_4_), channel_id=1, source_target_pairs={{0,2},{1,3},{2,0},{3,1},{4,6},{5,7},{6,4},{7,5},{8,10},{9,11},{10,... | collective-permute-start | bytes 393224 | tf_op jit(solution)/shard_map/ppermute | solution.py:225
  43.7 5.4 %collective-permute-start.14 = (f32[64,512]{1,0:T(8,128)S(1)}, f32[64,512]{1,0:T(8,128)S(1)}, u32[]{:S(2)}, u32[]{:S(2)}) collective-permute-start(f32[64,512]{1,0:T(8,128)S(1)} %shard_map.54.refs_10_.refs_0_), channel_id=1, source_target_pairs={{0,1},{1,0},{2,3},{3,2},{4,5},{5,4},{6,7},{7,6},{8,9},{9,8},{10,11... | collective-permute-start | bytes 393224 | tf_op jit(solution)/shard_map/ppermute | solution.py:225
  44.9 4.2 %collective-permute-start.18 = (f32[64,512]{1,0:T(8,128)S(1)}, f32[64,512]{1,0:T(8,128)S(1)}, u32[]{:S(2)}, u32[]{:S(2)}) collective-permute-start(f32[64,512]{1,0:T(8,128)S(1)} %collective-permute-done.17.refs_14_.refs_4_), channel_id=1, source_target_pairs={{0,1},{1,0},{2,3},{3,2},{4,5},{5,4},{6,7},{7,6},{8,9},{9,8},{10,11... | collective-permute-start | bytes 393224 | tf_op jit(solution)/shard_map/ppermute | solution.py:225
  45.2 5.9 %collective-permute-start.16 = (f32[64,512]{1,0:T(8,128)S(1)}, f32[64,512]{1,0:T(8,128)S(1)}, u32[]{:S(2)}, u32[]{:S(2)}) collective-permute-start(f32[64,512]{1,0:T(8,128)S(1)} %collective-permute-done.15.refs_12_.refs_2_), channel_id=1, source_target_pairs={{0,1},{1,0},{2,3},{3,2},{4,5},{5,4},{6,7},{7,6},{8,9},{9,8},{10,11... | collective-permute-start | bytes 393224 | tf_op jit(solution)/shard_map/ppermute | solution.py:225
  47.9 5.9 %collective-permute-start.20 = (f32[64,512]{1,0:T(8,128)S(1)}, f32[64,512]{1,0:T(8,128)S(1)}, u32[]{:S(2)}, u32[]{:S(2)}) collective-permute-start(f32[64,512]{1,0:T(8,128)S(1)} %collective-permute-done.19.refs_16_.refs_6_), channel_id=1, source_target_pairs={{0,1},{1,0},{2,3},{3,2},{4,5},{5,4},{6,7},{7,6},{8,9},{9,8},{10,11... | collective-permute-start | bytes 393224 | tf_op jit(solution)/shard_map/ppermute | solution.py:225
  54.3 7.0 %collective-permute-start.21 = (f32[256,256]{1,0:T(8,128)S(1)}, f32[256,256]{1,0:T(8,128)S(1)}, u32[]{:S(2)}, u32[]{:S(2)}) collective-permute-start(f32[256,256]{1,0:T(8,128)S(1)} %get-tuple-element.27), channel_id=1, source_target_pairs={{0,8},{1,9},{2,10},{3,11},{4,12},{5,13},{6,14},{7,15},{8,0},{9,1},... | collective-permute-start | bytes 786440 | tf_op jit(solution)/shard_map/ppermute | solution.py:225
  58.6 8.5 %collective-permute-start = (f32[256,256]{1,0:T(8,128)S(1)}, f32[256,256]{1,0:T(8,128)S(1)}, u32[]{:S(2)}, u32[]{:S(2)}) collective-permute-start(f32[256,256]{1,0:T(8,128)S(1)} %get-tuple-element.17.old_ref), channel_id=1, source_target_pairs={{0,16},{1,17},{2,18},{3,19},{4,20},{5,21},{6,22},{7,23},{8,24},{9,... | collective-permute-start | bytes 786440 | tf_op jit(solution)/shard_map/ppermute | solution.py:225
  59.8 8.1 %collective-permute-start.8 = (f32[256,256]{1,0:T(8,128)S(1)}, f32[256,256]{1,0:T(8,128)S(1)}, u32[]{:S(2)}, u32[]{:S(2)}) collective-permute-start(f32[256,256]{1,0:T(8,128)S(1)} %get-tuple-element.19), channel_id=1, source_target_pairs={{0,1},{1,0},{2,3},{3,2},{4,5},{5,4},{6,7},{7,6},{8,9},{9,8},{10,11... | collective-permute-start | bytes 786440 | tf_op jit(solution)/shard_map/ppermute | solution.py:225
  61.1 10.9 %collective-permute-start.6 = (f32[256,256]{1,0:T(8,128)S(1)}, f32[256,256]{1,0:T(8,128)S(1)}, u32[]{:S(2)}, u32[]{:S(2)}) collective-permute-start(f32[256,256]{1,0:T(8,128)S(1)} %get-tuple-element.18), channel_id=1, source_target_pairs={{0,16},{1,17},{2,18},{3,19},{4,20},{5,21},{6,22},{7,23},{8,24},{9,... | collective-permute-start | bytes 786440 | tf_op jit(solution)/shard_map/ppermute | solution.py:225
  61.3 13.7 %collective-permute-start.22 = (f32[64,256]{1,0:T(8,128)S(1)}, f32[64,256]{1,0:T(8,128)S(1)}, u32[]{:S(2)}, u32[]{:S(2)}) collective-permute-start(f32[64,256]{1,0:T(8,128)S(1)} %get-tuple-element.29), channel_id=1, source_target_pairs={{0,16},{1,17},{2,18},{3,19},{4,20},{5,21},{6,22},{7,23},{8,24},{9,... | collective-permute-start | bytes 196616 | tf_op jit(solution)/shard_map/ppermute | solution.py:225
  62.6 23.8 %collective-permute-start.5 = (f32[256,256]{1,0:T(8,128)S(1)}, f32[256,256]{1,0:T(8,128)S(1)}, u32[]{:S(2)}, u32[]{:S(2)}) collective-permute-start(f32[256,256]{1,0:T(8,128)S(1)} %get-tuple-element.18), channel_id=1, source_target_pairs={{0,0},{1,1},{2,8},{3,9},{4,4},{5,5},{6,6},{7,7},{8,2},{9,3},{10,10... | collective-permute-start | bytes 786440 | tf_op jit(solution)/shard_map/ppermute | solution.py:225
  67.1 19.3 %collective-permute-start.1 = (f32[256,256]{1,0:T(8,128)S(1)}, f32[256,256]{1,0:T(8,128)S(1)}, u32[]{:S(2)}, u32[]{:S(2)}) collective-permute-start(f32[256,256]{1,0:T(8,128)S(1)} %shard_map.51.old_ref), channel_id=1, source_target_pairs={{0,8},{1,9},{2,10},{3,11},{4,12},{5,13},{6,14},{7,15},{8,0},{9,1},... | collective-permute-start | bytes 786440 | tf_op jit(solution)/shard_map/ppermute | solution.py:225
  68.0 18.5 %collective-permute-start.9 = (f32[256,256]{1,0:T(8,128)S(1)}, f32[256,256]{1,0:T(8,128)S(1)}, u32[]{:S(2)}, u32[]{:S(2)}) collective-permute-start(f32[256,256]{1,0:T(8,128)S(1)} %collective-permute-done.8), channel_id=1, source_target_pairs={{0,0},{1,1},{2,8},{3,9},{4,16},{5,17},{6,24},{7,25},{8,2},{9,3},{1... | collective-permute-start | bytes 786440 | tf_op jit(solution)/shard_map/ppermute | solution.py:225
  72.0 14.5 %collective-permute-start.7 = (f32[256,256]{1,0:T(8,128)S(1)}, f32[256,256]{1,0:T(8,128)S(1)}, u32[]{:S(2)}, u32[]{:S(2)}) collective-permute-start(f32[256,256]{1,0:T(8,128)S(1)} %collective-permute-done.6), channel_id=1, source_target_pairs={{0,4},{1,5},{2,12},{3,13},{4,20},{5,21},{6,22},{7,23},{8,6},{9,7},... | collective-permute-start | bytes 786440 | tf_op jit(solution)/shard_map/ppermute | solution.py:225
  75.0 3.9 %collective-permute-start.23 = (f32[64,256]{1,0:T(8,128)S(1)}, f32[64,256]{1,0:T(8,128)S(1)}, u32[]{:S(2)}, u32[]{:S(2)}) collective-permute-start(f32[64,256]{1,0:T(8,128)S(1)} %get-tuple-element.30), channel_id=1, source_target_pairs={{0,1},{1,0},{2,3},{3,2},{4,5},{5,4},{6,7},{7,6},{8,9},{9,8},{10,11... | collective-permute-start | bytes 196616 | tf_op jit(solution)/shard_map/ppermute | solution.py:225
  78.9 4.4 %collective-permute-start.24 = (f32[64,256]{1,0:T(8,128)S(1)}, f32[64,256]{1,0:T(8,128)S(1)}, u32[]{:S(2)}, u32[]{:S(2)}) collective-permute-start(f32[64,256]{1,0:T(8,128)S(1)} %get-tuple-element.31), channel_id=1, source_target_pairs={{0,17},{1,16},{2,19},{3,18},{4,21},{5,20},{6,23},{7,22},{8,25},{9,... | collective-permute-start | bytes 196616 | tf_op jit(solution)/shard_map/ppermute | solution.py:225
  83.3 9.4 %collective-permute-start.25 = (f32[64,512]{1,0:T(8,128)S(1)}, f32[64,512]{1,0:T(8,128)S(1)}, u32[]{:S(2)}, u32[]{:S(2)}) collective-permute-start(f32[64,512]{1,0:T(8,128)S(1)} %shard_map.59), channel_id=1, source_target_pairs={{0,2},{1,3},{2,10},{3,11},{4,18},{5,19},{6,26},{7,27},{8,6},{9,7},... | collective-permute-start | bytes 393224 | tf_op jit(solution)/shard_map/ppermute | solution.py:225
